TPU v7x, 256 devices: a whole 4x4x8 slice. The times are simulated.
256 devices in a mesh: sec: 64 (over y, z, core), reg: 4 (over x).
Axes of the slice: x: 4, y: 4, z: 8, core: 2. Of those that a mesh axis runs over, the one named last changes fastest.
Arguments:
- start_params: float32 [64, 4, 20, 128], P('sec', 'reg'), may hold values from -3 to 3
- right_side: float32 [64, 4, 20, 128], P('sec', 'reg'), may hold values from -40 to 40
- prior: float32 [64, 4, 20, 128], P('sec', 'reg'), may hold values from 0.1 to 1
- matches: bfloat16 [64, 4, 640, 4, 256], P('sec', 'reg'), may hold values from -1 to 1
- pair_first: int32 [64, 4, 640], P('sec', 'reg'), may hold values from 0 to 127, as said below
- pair_second: int32 [64, 4, 640], P('sec', 'reg'), may hold values from 0 to 415, as said below
- match_counts: int32 [64, 4, 640], P('sec', 'reg'), may hold values from 0 to 256, as said below
- send_lists: int32 [64, 4, 2, 16], P('sec', 'reg'), may hold values from 0 to 127, as said below
Outputs:
- solution: float32 [64, 4, 20, 128], P('sec', 'reg')
- residual: float32 [64, 4, 20, 128], P('sec', 'reg')
Inputs may be any that keep to these rules, and one draw needn't show every extreme that they name: Each tile is pair_first of exactly five pairs of its device, in a drawn order. `pair_second`: names a column of the extended field; blocks of neighbours outside the grid are never named; a pair with match count 0 names its own tile. `match_counts`: 0 marks an absent pair; every device has a pair with exactly 256 matches. `send_lists`: row 0 holds the tiles whose coefficients a region lends to the region below it, row 1 to the region above; each row has 16 distinct tiles and the rows are disjoint.
All inputs are finite; a program needn't handle non-finite values.
Results may differ from a plain program's by a relative error of at most 0.0003.
Values sent between devices are 32-bit elements; how exact they have to be, the bound alone decides.
A program may use at most 64 MiB of HBM per device.

v0:
```python
import math

import jax
import jax.numpy as jnp
from jax import lax
from jax.sharding import PartitionSpec as P

FULL_PRECISION = lax.Precision.HIGHEST


def shifted(array, axis, by):
    length = lax.axis_size(axis)
    pairs = [(i, i + by) for i in range(length) if 0 <= i + by < length]
    return lax.ppermute(array, axis, pairs)


def padded_2(array, sides, width):
    for axis, dim in sides:
        size, length = (lax.axis_size(axis), array.shape[dim])
        up = [(i, (i + 1) % size) for i in range(size - 1)]
        down = [(j, i) for i, j in up]
        last = lax.slice_in_dim(array, length - width, length, axis=dim)
        first = lax.slice_in_dim(array, 0, width, axis=dim)
        before = lax.ppermute(last, axis, up)
        after = lax.ppermute(first, axis, down)
        array = jnp.concatenate([before, array, after], axis=dim)
    return array


def monomials(across, upward):
    constant = jnp.ones_like(across)
    square_a = across * across
    square_b = upward * upward
    mixed = across * upward
    return jnp.stack(
        [
            constant,
            across,
            upward,
            square_a,
            mixed,
            square_b,
            square_a * across,
            square_a * upward,
            square_b * across,
            square_b * upward,
        ]
    )


def match_bases(count_blk, match_blk):
    points = match_blk.astype(jnp.float32)
    slots = points.shape[-1]
    basis_a = monomials(points[:, 0], points[:, 1])
    basis_b = monomials(points[:, 2], points[:, 3])
    weights = jnp.where(jnp.arange(slots)[None, :] < count_blk[:, None], 2.0 / slots, 0.0).astype(
        jnp.float32
    )
    return (basis_a, basis_b, weights)


def block_terms(extended, first_blk, second_blk, count_blk, match_blk):
    width = first_blk.shape[0]
    basis_a, basis_b, weights = match_bases(count_blk, match_blk)
    own = jnp.take(extended, first_blk, axis=1).reshape(2, 10, width)
    other = jnp.take(extended, second_blk, axis=1).reshape(2, 10, width)
    mismatch = (
        jnp.einsum("mpk,cmp->cpk", basis_a, own, precision=FULL_PRECISION)
        - jnp.einsum("mpk,cmp->cpk", basis_b, other, precision=FULL_PRECISION)
    ) * weights[None]
    to_own = jnp.einsum("mpk,cpk->cmp", basis_a, mismatch, precision=FULL_PRECISION).reshape(
        20, width
    )
    to_other = -jnp.einsum("mpk,cpk->cmp", basis_b, mismatch, precision=FULL_PRECISION).reshape(
        20, width
    )
    return (to_own, to_other)


def split_blocks(first, second, counts, matches):
    pairs = first.shape[0]
    block = math.gcd(pairs, 512)
    blocks = pairs // block
    slots = matches.shape[-1]
    return (
        first.reshape(blocks, block),
        second.reshape(blocks, block),
        counts.reshape(blocks, block),
        matches.reshape(blocks, block, 4, slots),
    )


def extend(params, send_lists):
    arrived = params
    taken = []
    for hop_index in range(2):
        arrived = shifted(arrived, "sec", 1)
        taken.append(arrived)
    near_params, far_params = (taken[0], taken[1])
    faces = jnp.stack(
        [jnp.take(params, send_lists[0], axis=1), jnp.take(params, send_lists[1], axis=1)]
    )
    padded = padded_2(faces, (("reg", 0),), 1)
    return jnp.concatenate([params, near_params, far_params, padded[0], padded[3]], axis=1)


def fold_back(products, tiles, rows, send_lists):
    local = products[:, :tiles]
    near_part = products[:, tiles : 2 * tiles]
    far_part = products[:, 2 * tiles : 3 * tiles]
    outgoing = far_part
    arrived = far_part
    for hop_index in range(2):
        arrived = shifted(outgoing, "sec", -1)
        outgoing = near_part + arrived
    local = local + arrived
    faces = jnp.stack([products[:, 3 * tiles : 3 * tiles + rows], products[:, 3 * tiles + rows :]])
    padded = padded_2(faces, (("reg", 0),), 1)
    local = local.at[:, send_lists[0]].add(padded[0])
    return local.at[:, send_lists[1]].add(padded[3])


def apply_normal(params, prior, first, second, counts, matches, send_lists):
    tiles = params.shape[1]
    rows = send_lists.shape[1]
    pairs = first.shape[0]
    extended = extend(params, send_lists)
    pieces = split_blocks(first, second, counts, matches)
    to_own, to_other = lax.map(
        lambda items: block_terms(extended, items[0], items[1], items[2], items[3]), pieces
    )
    to_own = jnp.moveaxis(to_own, 0, 1).reshape(20, pairs)
    to_other = jnp.moveaxis(to_other, 0, 1).reshape(20, pairs)
    products = jnp.zeros((20, extended.shape[1]), jnp.float32)
    products = products.at[:, first].add(to_own).at[:, second].add(to_other)
    return fold_back(products, tiles, rows, send_lists) + prior * params


def global_dot(value):
    return lax.psum(value, ("sec", "reg"))


def on_device(
    start_params, right_side, prior, matches, pair_first, pair_second, match_counts, send_lists
):
    params_start = start_params[0, 0]
    target = right_side[0, 0]
    damping = prior[0, 0]
    first = pair_first[0, 0]
    second = pair_second[0, 0]
    counts = match_counts[0, 0]
    points = matches[0, 0]
    border = send_lists[0, 0]

    def normal(field):
        return apply_normal(field, damping, first, second, counts, points, border)

    solution = params_start
    residual = target - normal(params_start)
    direction = residual
    norm_now = global_dot(jnp.sum(residual * residual))
    image = normal(direction)
    alpha = norm_now / global_dot(jnp.sum(direction * image))
    solution = solution + alpha * direction
    residual = residual - alpha * image
    return (solution[None, None], residual[None, None])


def solution(mesh):
    return jax.shard_map(
        on_device,
        mesh=mesh,
        in_specs=(
            P("sec", "reg", None, None),
            P("sec", "reg", None, None),
            P("sec", "reg", None, None),
            P("sec", "reg", None, None, None),
            P("sec", "reg", None),
            P("sec", "reg", None),
            P("sec", "reg", None),
            P("sec", "reg", None, None),
        ),
        out_specs=(P("sec", "reg", None, None), P("sec", "reg", None, None)),
        check_vma=False,
    )
```

profile of v0, /device:TPU:1, one launch (start us, length us, event | category | flops | bytes accessed | tf_op | source)
XLA Modules:
  0.0 496.9 jit_solution(6133939188612458602)
XLA Ops:
  1.4 4.9 collective-permute-start
  7.8 3.1 collective-permute-start.2
  23.0 152.0 %while.24 = (s32[]{:T(128)}, f32[5,20,128]{2,1,0:T(8,128)}, f32[5,20,128]{2,1,0:T(8,128)}, s32[5,128]{1,0:T(8,128)S(1)}, f32[20,416]{0,1:T(8,128)}, /*index=5*/b...) while((s32[]{:T(128)}, f32[5,20,128]{2,1,0:T(8,128)}, ...), condition=%wide.region_1.4_spmd, body=%wide.region_0.3_spmd.sunk | while | flops 32287744 | bytes 16952436 | solution.py:129
  27.2 4.8 stack.53
  32.7 5.4 %stack.52 = f32[10,128,256]{2,0,1:T(8,128)} concatenate(f32[1,128,256]{2,0,1:T(1,128)S(1)} %broadcast.300, f32[1,128,256]{2,0,1:T(1,128)} %get-tuple-element.348, f32[1,128,256]{2,0,1:T(1,128)} %get-tuple-element.349, f32[1,128,256]{2,0,1:T(1,128)S(1)} %get-tuple-element.350, f32[1,128,256]{2,0,1:T(1,128)S(1)} %get-tuple-element.351, f32[1,128,256]{2,0,1:T(1,128)S(1)} %get-tuple-element.352, ...), dimensions={0} | concatenate | bytes 2621440 | tf_op jit(solution)/shard_map/while/body/eval_jaxpr/stack | solution.py:35
  40.0 2.8 fusion.96
  49.3 3.4 convolution_bitcast_fusion.4
  57.5 4.8 stack.53
  63.1 5.4 %stack.52 = f32[10,128,256]{2,0,1:T(8,128)} concatenate(f32[1,128,256]{2,0,1:T(1,128)S(1)} %broadcast.300, f32[1,128,256]{2,0,1:T(1,128)} %get-tuple-element.348, f32[1,128,256]{2,0,1:T(1,128)} %get-tuple-element.349, f32[1,128,256]{2,0,1:T(1,128)S(1)} %get-tuple-element.350, f32[1,128,256]{2,0,1:T(1,128)S(1)} %get-tuple-element.351, f32[1,128,256]{2,0,1:T(1,128)S(1)} %get-tuple-element.352, ...), dimensions={0} | concatenate | bytes 2621440 | tf_op jit(solution)/shard_map/while/body/eval_jaxpr/stack | solution.py:35
  79.7 3.4 convolution_bitcast_fusion.4
  87.9 4.8 stack.53
  93.5 5.4 %stack.52 = f32[10,128,256]{2,0,1:T(8,128)} concatenate(f32[1,128,256]{2,0,1:T(1,128)S(1)} %broadcast.300, f32[1,128,256]{2,0,1:T(1,128)} %get-tuple-element.348, f32[1,128,256]{2,0,1:T(1,128)} %get-tuple-element.349, f32[1,128,256]{2,0,1:T(1,128)S(1)} %get-tuple-element.350, f32[1,128,256]{2,0,1:T(1,128)S(1)} %get-tuple-element.351, f32[1,128,256]{2,0,1:T(1,128)S(1)} %get-tuple-element.352, ...), dimensions={0} | concatenate | bytes 2621440 | tf_op jit(solution)/shard_map/while/body/eval_jaxpr/stack | solution.py:35
  110.0 3.4 convolution_bitcast_fusion.4
  118.3 4.8 stack.53
  123.9 5.4 %stack.52 = f32[10,128,256]{2,0,1:T(8,128)} concatenate(f32[1,128,256]{2,0,1:T(1,128)S(1)} %broadcast.300, f32[1,128,256]{2,0,1:T(1,128)} %get-tuple-element.348, f32[1,128,256]{2,0,1:T(1,128)} %get-tuple-element.349, f32[1,128,256]{2,0,1:T(1,128)S(1)} %get-tuple-element.350, f32[1,128,256]{2,0,1:T(1,128)S(1)} %get-tuple-element.351, f32[1,128,256]{2,0,1:T(1,128)S(1)} %get-tuple-element.352, ...), dimensions={0} | concatenate | bytes 2621440 | tf_op jit(solution)/shard_map/while/body/eval_jaxpr/stack | solution.py:35
  140.5 3.4 convolution_bitcast_fusion.4
  148.7 4.8 stack.53
  154.3 5.4 %stack.52 = f32[10,128,256]{2,0,1:T(8,128)} concatenate(f32[1,128,256]{2,0,1:T(1,128)S(1)} %broadcast.300, f32[1,128,256]{2,0,1:T(1,128)} %get-tuple-element.348, f32[1,128,256]{2,0,1:T(1,128)} %get-tuple-element.349, f32[1,128,256]{2,0,1:T(1,128)S(1)} %get-tuple-element.350, f32[1,128,256]{2,0,1:T(1,128)S(1)} %get-tuple-element.351, f32[1,128,256]{2,0,1:T(1,128)S(1)} %get-tuple-element.352, ...), dimensions={0} | concatenate | bytes 2621440 | tf_op jit(solution)/shard_map/while/body/eval_jaxpr/stack | solution.py:35
  170.8 3.4 convolution_bitcast_fusion.4
  177.2 6.4 %scatter_custom_fusion = f32[20,416]{0,1:T(8,128)S(1)} fusion(s32[640]{0:T(1024)} %fusion.40, f32[640,20]{1,0:T(8,128)S(1)} %copy.78, f32[]{:T(128)} %constant.56.clone.1), kind=kCustom, calls=%fused_computation.104 | custom fusion | flops 12800 | bytes 33792 | tf_op jit(solution)/shard_map/scatter-add | solution.py:135
  183.6 6.1 %scatter_fusion = f32[20,416]{0,1:T(8,128)S(1)} fusion(f32[20,416]{0,1:T(8,128)S(1)} %scatter_custom_fusion, s32[640]{0:T(1024)S(1)} %fusion.41, f32[640,20]{1,0:T(8,128)S(1)} %copy.80), kind=kCustom, calls=%fused_computation.9 | custom fusion | flops 12800 | bytes 156160 | tf_op jit(solution)/shard_map/scatter-add | solution.py:135
  192.1 3.2 collective-permute-done.4
  197.2 4.3 collective-permute-start.6
  206.6 5.1 %collective-permute-start.8 = (f32[20,128]{0,1:T(8,128)S(1)}, f32[20,128]{0,1:T(8,128)S(1)}, u32[]{:S(2)}, u32[]{:S(2)}) collective-permute-start(f32[20,128]{0,1:T(8,128)S(1)} %bitcast_subtract_fusion), channel_id=1, source_target_pairs={{0,4},{4,8},{8,12},{12,16},{16,20},{20,24},{24,28},{28,32},{32,36}... | collective-permute-start | bytes 30728 | tf_op jit(solution)/shard_map/ppermute | solution.py:14
  213.0 3.1 collective-permute-start.10
  219.9 2.9 collective-permute-done.11
  225.3 152.0 %while.25 = (s32[]{:T(128)}, f32[5,20,128]{2,1,0:T(8,128)}, f32[5,20,128]{2,1,0:T(8,128)}, s32[5,128]{1,0:T(8,128)S(1)}, f32[20,416]{0,1:T(8,128)}, /*index=5*/b...) while((s32[]{:T(128)}, f32[5,20,128]{2,1,0:T(8,128)}, ...), condition=%wide.region_9.12_spmd, body=%wide.region_8.11_spmd.sunk | while | flops 32287744 | bytes 16952436 | solution.py:129
  229.5 4.8 stack.71
  235.1 5.4 %stack.70 = f32[10,128,256]{2,0,1:T(8,128)} concatenate(f32[1,128,256]{2,0,1:T(1,128)S(1)} %broadcast.309, f32[1,128,256]{2,0,1:T(1,128)} %get-tuple-element.377, f32[1,128,256]{2,0,1:T(1,128)} %get-tuple-element.378, f32[1,128,256]{2,0,1:T(1,128)S(1)} %get-tuple-element.379, f32[1,128,256]{2,0,1:T(1,128)S(1)} %get-tuple-element.380, f32[1,128,256]{2,0,1:T(1,128)S(1)} %get-tuple-element.381, ...), dimensions={0} | concatenate | bytes 2621440 | tf_op jit(solution)/shard_map/while/body/eval_jaxpr/stack | solution.py:35
  251.6 3.4 convolution_bitcast_fusion.5
  259.9 4.8 stack.71
  265.5 5.4 %stack.70 = f32[10,128,256]{2,0,1:T(8,128)} concatenate(f32[1,128,256]{2,0,1:T(1,128)S(1)} %broadcast.309, f32[1,128,256]{2,0,1:T(1,128)} %get-tuple-element.377, f32[1,128,256]{2,0,1:T(1,128)} %get-tuple-element.378, f32[1,128,256]{2,0,1:T(1,128)S(1)} %get-tuple-element.379, f32[1,128,256]{2,0,1:T(1,128)S(1)} %get-tuple-element.380, f32[1,128,256]{2,0,1:T(1,128)S(1)} %get-tuple-element.381, ...), dimensions={0} | concatenate | bytes 2621440 | tf_op jit(solution)/shard_map/while/body/eval_jaxpr/stack | solution.py:35
  282.0 3.4 convolution_bitcast_fusion.5
  290.3 4.8 stack.71
  295.8 5.4 %stack.70 = f32[10,128,256]{2,0,1:T(8,128)} concatenate(f32[1,128,256]{2,0,1:T(1,128)S(1)} %broadcast.309, f32[1,128,256]{2,0,1:T(1,128)} %get-tuple-element.377, f32[1,128,256]{2,0,1:T(1,128)} %get-tuple-element.378, f32[1,128,256]{2,0,1:T(1,128)S(1)} %get-tuple-element.379, f32[1,128,256]{2,0,1:T(1,128)S(1)} %get-tuple-element.380, f32[1,128,256]{2,0,1:T(1,128)S(1)} %get-tuple-element.381, ...), dimensions={0} | concatenate | bytes 2621440 | tf_op jit(solution)/shard_map/while/body/eval_jaxpr/stack | solution.py:35
  312.4 3.4 convolution_bitcast_fusion.5
  320.6 4.8 stack.71
  326.2 5.4 %stack.70 = f32[10,128,256]{2,0,1:T(8,128)} concatenate(f32[1,128,256]{2,0,1:T(1,128)S(1)} %broadcast.309, f32[1,128,256]{2,0,1:T(1,128)} %get-tuple-element.377, f32[1,128,256]{2,0,1:T(1,128)} %get-tuple-element.378, f32[1,128,256]{2,0,1:T(1,128)S(1)} %get-tuple-element.379, f32[1,128,256]{2,0,1:T(1,128)S(1)} %get-tuple-element.380, f32[1,128,256]{2,0,1:T(1,128)S(1)} %get-tuple-element.381, ...), dimensions={0} | concatenate | bytes 2621440 | tf_op jit(solution)/shard_map/while/body/eval_jaxpr/stack | solution.py:35
  342.8 3.4 convolution_bitcast_fusion.5
  351.0 4.8 stack.71
  356.6 5.4 %stack.70 = f32[10,128,256]{2,0,1:T(8,128)} concatenate(f32[1,128,256]{2,0,1:T(1,128)S(1)} %broadcast.309, f32[1,128,256]{2,0,1:T(1,128)} %get-tuple-element.377, f32[1,128,256]{2,0,1:T(1,128)} %get-tuple-element.378, f32[1,128,256]{2,0,1:T(1,128)S(1)} %get-tuple-element.379, f32[1,128,256]{2,0,1:T(1,128)S(1)} %get-tuple-element.380, f32[1,128,256]{2,0,1:T(1,128)S(1)} %get-tuple-element.381, ...), dimensions={0} | concatenate | bytes 2621440 | tf_op jit(solution)/shard_map/while/body/eval_jaxpr/stack | solution.py:35
  373.1 3.4 convolution_bitcast_fusion.5
  379.4 6.4 %scatter_custom_fusion.4 = f32[20,416]{0,1:T(8,128)S(1)} fusion(s32[640]{0:T(1024)} %fusion.40, f32[640,20]{1,0:T(8,128)S(1)} %copy.89, f32[]{:T(128)} %constant.56.clone.1), kind=kCustom, calls=%fused_computation.102 | custom fusion | flops 12800 | bytes 33792 | tf_op jit(solution)/shard_map/scatter-add | solution.py:135
  385.9 6.1 %scatter_fusion.1 = f32[20,416]{0,1:T(8,128)S(1)} fusion(f32[20,416]{0,1:T(8,128)S(1)} %scatter_custom_fusion.4, s32[640]{0:T(1024)S(1)} %fusion.41, f32[640,20]{1,0:T(8,128)S(1)} %copy.91), kind=kCustom, calls=%fused_computation.13 | custom fusion | flops 12800 | bytes 156160 | tf_op jit(solution)/shard_map/scatter-add | solution.py:135
  392.0 3.3 collective-permute-start.12
  395.3 3.5 collective-permute-done.12
  400.8 2.8 collective-permute-start.14
  409.4 84.8 %all-reduce = (f32[]{:T(128)}, f32[]{:T(128)}) all-reduce(f32[]{:T(128)} %get-tuple-element.119, f32[]{:T(128)} %get-tuple-element.118), channel_id=1, replica_groups=mesh['sec'=64,'reg'=4] {'sec','reg'}, use_global_device_ids=true, to_apply=%region_7.10 | all-reduce | flops 2 | bytes 16 | tf_op jit(solution)/shard_map/psum | solution.py:140
  (376 shorter events, 208.0 us)
Async XLA Ops:
  1.4 21.6 %copy-start.2 = (f32[1,1,20,128]{2,3,1,0:T(8,128)}, f32[1,1,20,128]{2,3,1,0:T(8,128)S(1)}, u32[]{:S(2)}) copy-start(f32[1,1,20,128]{2,3,1,0:T(8,128)S(1)} %copy.69) | copy-start | bytes 30724
  1.4 12.7 %collective-permute-start = (f32[20,128]{0,1:T(8,128)S(1)}, f32[20,128]{0,1:T(8,128)S(1)}, u32[]{:S(2)}, u32[]{:S(2)}) collective-permute-start(f32[20,128]{0,1:T(8,128)S(1)} %bitcast.359), channel_id=1, source_target_pairs={{0,4},{4,8},{8,12},{12,16},{16,20},{20,24},{24,28},{28,32},{32,36}... | collective-permute-start | bytes 30728 | tf_op jit(solution)/shard_map/ppermute | solution.py:14
  7.1 3.8 copy-start.12
  7.1 13.3 %copy-start.10 = (pred[16]{0:T(512)(128)(4,1)}, pred[16]{0:T(512)(128)(4,1)S(1)}, u32[]{:S(2)}) copy-start(pred[16]{0:T(512)(128)(4,1)S(1)} %get-tuple-element.162) | copy-start | bytes 52
  7.8 12.7 %collective-permute-start.2 = (f32[1,20,16]{1,2,0:T(8,128)S(1)}, f32[1,20,16]{1,2,0:T(8,128)S(1)}, u32[]{:S(2)}, u32[]{:S(2)}) collective-permute-start(f32[1,20,16]{1,2,0:T(8,128)S(1)} %select_bitcast_fusion.7), channel_id=1, source_target_pairs={{0,1},{1,2},{2,3},{4,5},{5,6},{6,7},{8,9},{9,10},{10,11},{12,13},{... | collective-permute-start | bytes 3848 | tf_op jit(solution)/shard_map/ppermute | solution.py:24
  10.9 9.6 %copy-start.9 = (s32[1024]{0:T(1024)}, s32[1024]{0:T(1024)S(1)}, u32[]{:S(2)}) copy-start(s32[1024]{0:T(1024)S(1)} %pad_clamp_fusion.4) | copy-start | bytes 12292
  11.6 9.0 %collective-permute-start.3 = (f32[1,20,16]{1,2,0:T(8,128)S(1)}, f32[1,20,16]{1,2,0:T(8,128)S(1)}, u32[]{:S(2)}, u32[]{:S(2)}) collective-permute-start(f32[1,20,16]{1,2,0:T(8,128)S(1)} %select_bitcast_fusion.6), channel_id=1, source_target_pairs={{1,0},{2,1},{3,2},{5,4},{6,5},{7,6},{9,8},{10,9},{11,10},{13,12},{... | collective-permute-start | bytes 3848 | tf_op jit(solution)/shard_map/ppermute | solution.py:25
  14.2 6.5 %collective-permute-start.1 = (f32[20,128]{0,1:T(8,128)S(1)}, f32[20,128]{0,1:T(8,128)S(1)}, u32[]{:S(2)}, u32[]{:S(2)}) collective-permute-start(f32[20,128]{0,1:T(8,128)S(1)} %collective-permute-done), channel_id=1, source_target_pairs={{0,4},{4,8},{8,12},{12,16},{16,20},{20,24},{24,28},{28,32},{32,36}... | collective-permute-start | bytes 30728 | tf_op jit(solution)/shard_map/ppermute | solution.py:14
  175.0 16.9 %copy-start.14 = (s32[1,1,2,16]{3,2,1,0:T(2,128)S(1)}, s32[1,1,2,16]{3,2,1,0:T(2,128)}, u32[]{:S(2)}) copy-start(s32[1,1,2,16]{3,2,1,0:T(2,128)} %param.23) | copy-start | bytes 388
  175.0 16.9 %copy-start.7 = (f32[1,1,20,128]{3,1,2,0:T(1,128)S(1)}, f32[1,1,20,128]{3,1,2,0:T(1,128)}, u32[]{:S(2)}) copy-start(f32[1,1,20,128]{3,1,2,0:T(1,128)} %param.18) | copy-start | bytes 30724
  175.0 17.0 %copy-start.8 = (f32[1,1,20,128]{3,1,2,0:T(1,128)S(1)}, f32[1,1,20,128]{3,1,2,0:T(1,128)}, u32[]{:S(2)}) copy-start(f32[1,1,20,128]{3,1,2,0:T(1,128)} %param.17) | copy-start | bytes 30724
  175.0 27.8 %copy-start.3 = (f32[1,1,20,128]{2,3,1,0:T(8,128)S(1)}, f32[1,1,20,128]{2,3,1,0:T(8,128)}, u32[]{:S(2)}) copy-start(f32[1,1,20,128]{2,3,1,0:T(8,128)} %copy-done.2) | copy-start | bytes 30724
  175.9 36.4 %copy-start.13 = (pred[16]{0:T(512)(128)(4,1)S(1)}, pred[16]{0:T(512)(128)(4,1)}, u32[]{:S(2)}) copy-start(pred[16]{0:T(512)(128)(4,1)} %copy-done.12) | copy-start | bytes 52
  175.9 42.5 %copy-start.11 = (pred[16]{0:T(512)(128)(4,1)S(1)}, pred[16]{0:T(512)(128)(4,1)}, u32[]{:S(2)}) copy-start(pred[16]{0:T(512)(128)(4,1)} %copy-done.10) | copy-start | bytes 52
  189.7 5.6 %collective-permute-start.4 = (f32[20,128]{0,1:T(8,128)S(1)}, f32[20,128]{0,1:T(8,128)S(1)}, u32[]{:S(2)}, u32[]{:S(2)}) collective-permute-start(f32[20,128]{0,1:T(8,128)S(1)} %slice.106), channel_id=1, source_target_pairs={{4,0},{8,4},{12,8},{16,12},{20,16},{24,20},{28,24},{32,28},{36,32}... | collective-permute-start | bytes 30728 | tf_op jit(solution)/shard_map/ppermute | solution.py:14
  191.9 33.4 %copy-start.15 = (s32[16]{0:T(128)}, s32[16]{0:T(128)S(1)}, u32[]{:S(2)}) copy-start(s32[16]{0:T(128)S(1)} %get-tuple-element.210) | copy-start | bytes 196
  191.9 33.4 %copy-start.16 = (s32[16]{0:T(128)}, s32[16]{0:T(128)S(1)}, u32[]{:S(2)}) copy-start(s32[16]{0:T(128)S(1)} %get-tuple-element.211) | copy-start | bytes 196
  192.0 33.3 %copy-start.5 = (f32[1,1,20,128]{2,3,1,0:T(8,128)}, f32[1,1,20,128]{2,3,1,0:T(8,128)S(1)}, u32[]{:S(2)}) copy-start(f32[1,1,20,128]{2,3,1,0:T(8,128)S(1)} %copy.81) | copy-start | bytes 30724
  195.3 7.5 %collective-permute-start.5 = (f32[20,128]{0,1:T(8,128)S(1)}, f32[20,128]{0,1:T(8,128)S(1)}, u32[]{:S(2)}, u32[]{:S(2)}) collective-permute-start(f32[20,128]{0,1:T(8,128)S(1)} %slice_add_fusion.2), channel_id=1, source_target_pairs={{4,0},{8,4},{12,8},{16,12},{20,16},{24,20},{28,24},{32,28},{36,32}... | collective-permute-start | bytes 30728 | tf_op jit(solution)/shard_map/ppermute | solution.py:14
  197.2 5.6 %collective-permute-start.6 = (f32[1,20,16]{1,2,0:T(8,128)S(1)}, f32[1,20,16]{1,2,0:T(8,128)S(1)}, u32[]{:S(2)}, u32[]{:S(2)}) collective-permute-start(f32[1,20,16]{1,2,0:T(8,128)S(1)} %get-tuple-element.207), channel_id=1, source_target_pairs={{0,1},{1,2},{2,3},{4,5},{5,6},{6,7},{8,9},{9,10},{10,11},{12,13},{... | collective-permute-start | bytes 3848 | tf_op jit(solution)/shard_map/ppermute | solution.py:24
  201.5 4.4 collective-permute-start.7
  206.6 18.7 %copy-start = (f32[20,128]{0,1:T(8,128)}, f32[20,128]{0,1:T(8,128)S(1)}, u32[]{:S(2)}) copy-start(f32[20,128]{0,1:T(8,128)S(1)} %bitcast_subtract_fusion) | copy-start | bytes 30724
  206.6 9.5 %collective-permute-start.8 = (f32[20,128]{0,1:T(8,128)S(1)}, f32[20,128]{0,1:T(8,128)S(1)}, u32[]{:S(2)}, u32[]{:S(2)}) collective-permute-start(f32[20,128]{0,1:T(8,128)S(1)} %bitcast_subtract_fusion), channel_id=1, source_target_pairs={{0,4},{4,8},{8,12},{12,16},{16,20},{20,24},{24,28},{28,32},{32,36}... | collective-permute-start | bytes 30728 | tf_op jit(solution)/shard_map/ppermute | solution.py:14
  213.0 6.8 %collective-permute-start.10 = (f32[1,20,16]{1,2,0:T(8,128)S(1)}, f32[1,20,16]{1,2,0:T(8,128)S(1)}, u32[]{:S(2)}, u32[]{:S(2)}) collective-permute-start(f32[1,20,16]{1,2,0:T(8,128)S(1)} %select_bitcast_fusion.5), channel_id=1, source_target_pairs={{0,1},{1,2},{2,3},{4,5},{5,6},{6,7},{8,9},{9,10},{10,11},{12,13},{... | collective-permute-start | bytes 3848 | tf_op jit(solution)/shard_map/ppermute | solution.py:24
  216.2 6.8 %collective-permute-start.9 = (f32[20,128]{0,1:T(8,128)S(1)}, f32[20,128]{0,1:T(8,128)S(1)}, u32[]{:S(2)}, u32[]{:S(2)}) collective-permute-start(f32[20,128]{0,1:T(8,128)S(1)} %collective-permute-done.8), channel_id=1, source_target_pairs={{0,4},{4,8},{8,12},{12,16},{16,20},{20,24},{24,28},{28,32},{32,36}... | collective-permute-start | bytes 30728 | tf_op jit(solution)/shard_map/ppermute | solution.py:14
  218.5 4.4 collective-permute-start.11
  377.3 27.6 %copy-start.1 = (f32[20,128]{0,1:T(8,128)S(1)}, f32[20,128]{0,1:T(8,128)}, u32[]{:S(2)}) copy-start(f32[20,128]{0,1:T(8,128)} %copy-done) | copy-start | bytes 30724
  377.3 27.6 %copy-start.6 = (f32[1,1,20,128]{2,3,1,0:T(8,128)S(1)}, f32[1,1,20,128]{2,3,1,0:T(8,128)}, u32[]{:S(2)}) copy-start(f32[1,1,20,128]{2,3,1,0:T(8,128)} %copy-done.5) | copy-start | bytes 30724
  377.3 118.3 %copy-start.4 = (f32[1,1,20,128]{2,3,1,0:T(8,128)S(1)}, f32[1,1,20,128]{2,3,1,0:T(8,128)}, u32[]{:S(2)}) copy-start(f32[1,1,20,128]{2,3,1,0:T(8,128)} %copy-done.2) | copy-start | bytes 30724
  392.0 6.8 %collective-permute-start.12 = (f32[20,128]{0,1:T(8,128)S(1)}, f32[20,128]{0,1:T(8,128)S(1)}, u32[]{:S(2)}, u32[]{:S(2)}) collective-permute-start(f32[20,128]{0,1:T(8,128)S(1)} %slice.111), channel_id=1, source_target_pairs={{4,0},{8,4},{12,8},{16,12},{20,16},{24,20},{28,24},{32,28},{36,32}... | collective-permute-start | bytes 30728 | tf_op jit(solution)/shard_map/ppermute | solution.py:14
  398.8 6.1 %collective-permute-start.13 = (f32[20,128]{0,1:T(8,128)S(1)}, f32[20,128]{0,1:T(8,128)S(1)}, u32[]{:S(2)}, u32[]{:S(2)}) collective-permute-start(f32[20,128]{0,1:T(8,128)S(1)} %slice_add_fusion), channel_id=1, source_target_pairs={{4,0},{8,4},{12,8},{16,12},{20,16},{24,20},{28,24},{32,28},{36,32}... | collective-permute-start | bytes 30728 | tf_op jit(solution)/shard_map/ppermute | solution.py:14
  400.8 4.2 collective-permute-start.14
  403.6 4.4 collective-permute-start.15
where the time goes:
time: 506 us; the launch traced here: 497 us
  local copies, waits for them, and re-layouts  185 us (37%)
  matrix products  93.3 us (18%)
  blocking collectives  84.8 us (17%)
  other arithmetic  74.4 us (15%)
  starting transfers between devices  42.1 us (8%)
  waiting for transfers between devices  14.2 us (3%)
    another operation x20, local copies, waits for them, and re-layouts, monomials(): jnp.stack([constant, across, upward, square_a, mixed, square_b, square_a...  102 us
    psum x1, blocking collectives, global_dot(): return lax.psum(value, ('sec', 'reg'))  84.8 us
    dot_general x10, matrix products, block_terms(): jnp.einsum('mpk,cpk->cmp', basis_a, mismatch, precision=FULL_PRECISION)  34.1 us
    dot_general x10, matrix products, block_terms(): jnp.einsum('mpk,cmp->cpk', basis_a, own, precision=FULL_PRECISION)  27.9 us
    scatter-add x4, other arithmetic, apply_normal(): products = products.at[:, first].add(to_own).at[:, second].add(to_other)  25 us
    ppermute x8, starting transfers between devices, shifted(): return lax.ppermute(array, axis, pairs)  23.6 us
    mul x10, other arithmetic, monomials(): square_b * upward  19.2 us
    dot_general x10, matrix products, block_terms(): jnp.einsum('mpk,cpk->cmp', basis_b, mismatch, precision=FULL_PRECISION)  18.3 us
  transfers between devices with their start and end apart: 16, of which 5 were waited for; matrix products, arithmetic and copies ran while one was open for 2% of the time, Pallas kernels for 0%

commit v1 on v0

v1 whole, which is shorter than its diff:
```python
import functools

import jax
import jax.numpy as jnp
from jax import lax
from jax.experimental import pallas as pl
from jax.experimental.pallas import tpu as pltpu
from jax.sharding import PartitionSpec as P

F32, BF16 = jnp.float32, jnp.bfloat16
MESH = pl.DeviceIdType.MESH
EXPONENTS = [(0, 0), (1, 0), (0, 1), (2, 0), (1, 1), (0, 2), (3, 0), (2, 1), (1, 2), (0, 3)]
MOMENTS = [(i, d - i) for d in range(1, 7) for i in range(d, -1, -1)]
TILES = 128
LANES = 128
FIELD = 32
UNROLL = 8


def powers(x, y):
    x2, xy, y2 = x * x, x * y, y * y
    return [None, x, y, x2, xy, y2, x2 * x, x2 * y, y2 * x, y2 * y]


def moments(x, y):
    base = dict(zip(EXPONENTS, powers(x, y)))
    known = dict(base)
    for i, j in MOMENTS:
        if (i, j) not in known:
            a = next(e for e in EXPONENTS[:2:-1] if (i - e[0], j - e[1]) in base)
            known[i, j] = base[a] * base[i - a[0], j - a[1]]
    return [known[e] for e in MOMENTS]


def row_of(n):
    return 16 * (n // 10) + n % 10


def gram_tile(coords, gram, tile, count, slots):
    zero = jnp.zeros((8, LANES), F32)
    gram[tile, :, 8:16, :] = jnp.zeros((20, 8, LANES), F32)
    gram[tile, :, 24:32, :] = jnp.zeros((20, 8, LANES), F32)

    def sums(terms, which):
        def step(i, totals):
            for u in range(UNROLL):
                at = pl.multiple_of((i * UNROLL + u) * 8, 8)
                new = terms(*[coords[c, pl.ds(at, 8), :] for c in which])
                totals = tuple(a + b for a, b in zip(totals, new))
            return totals

        totals = lax.fori_loop(0, slots // 8 // UNROLL, step, (zero,) * 27)
        return [jnp.sum(t, axis=0, keepdims=True) for t in totals]

    def put(n, m, row):
        r = row_of(m)
        gram[tile, n, r : r + 1, :] = row

    for side in range(2):
        table = dict(zip(MOMENTS, sums(moments, (2 * side, 2 * side + 1))))
        table[0, 0] = count
        for n, (i, j) in enumerate(EXPONENTS):
            for m, (k, l) in enumerate(EXPONENTS):
                put(10 * side + n, 10 * side + m, table[i + k, j + l])
        for n, e in enumerate(EXPONENTS):
            if side == 1:
                put(0, 10 + n, table[e])
                put(10 + n, 0, table[e])
            elif n:
                put(10, n, table[e])
                put(n, 10, table[e])
    for group in range(3):
        some = range(1 + 3 * group, 4 + 3 * group)

        def terms(xa, ya, xb, yb):
            a, b = powers(xa, ya), powers(xb, yb)
            return [a[m] * b[n] for m in some for n in range(1, 10)]

        rows = iter(sums(terms, (0, 1, 2, 3)))
        for m in some:
            for n in range(1, 10):
                row = next(rows)
                put(m, 10 + n, row)
                put(10 + n, m, row)


def thirds(x):
    high = x.astype(BF16)
    rest = x - high.astype(F32)
    middle = rest.astype(BF16)
    low = (rest - middle.astype(F32)).astype(BF16)
    return jnp.concatenate([high, middle, low], axis=0)


def joined(x):
    rows = x.shape[0] // 3
    return x[:rows] + x[rows : 2 * rows] + x[2 * rows :]


def matmul(a, b):
    return lax.dot_general(a, b, (((1,), (0,)), ((), ())), preferred_element_type=F32)


def matmul_t(a, b):
    return lax.dot_general(a, b, (((1,), (1,)), ((), ())), preferred_element_type=F32)


def kernel(
    sizes, params_hbm, side_hbm, prior_hbm, matches_hbm, first_ref, second_ref, count_ref, lists_ref,
    solution_ref, residual_ref,
    params, side, prior, points, coords, gram, own_hot, other_hot, z_ref,
    direction, lists_in, halo_in, fold_out, fold_in, part, part_in,
    load_sem, field_sem, list_send, list_recv, halo_send, halo_recv, fold_send, fold_recv, part_send, part_recv,
):
    secs, regs, group = sizes
    sec, reg = lax.axis_index("sec"), lax.axis_index("reg")
    pairs = first_ref.shape[1]
    slots = matches_hbm.shape[2]
    chunks = pairs // LANES
    rows = secs // group
    part_count = rows * regs

    def device(by_sec, by_reg):
        return (lax.rem(sec + by_sec + secs, secs), lax.rem(reg + by_reg + regs, regs))

    borrowers = [device(1, 0), device(2, 0), device(0, 1), device(0, -1)]
    owners = [device(-1, 0), device(-2, 0), device(0, -1), device(0, 1)]
    base, place = group * (sec // group), lax.rem(sec, group)
    line = [(base + lax.rem(place + j, group), reg) for j in range(1, group)]
    here = (sec // group) * regs + reg
    plane = []
    for j in range(1, part_count):
        there = lax.rem(here + j, part_count)
        plane.append(((there // regs) * group + place, lax.rem(there, regs)))

    barrier = pltpu.get_barrier_semaphore()
    for peer in borrowers + owners[:2] + line + plane:
        pl.semaphore_signal(barrier, inc=1, device_id=peer, device_id_type=MESH)

    loads = []
    for i in range(chunks):
        loads.append(pltpu.make_async_copy(matches_hbm.at[pl.ds(i * LANES, LANES)], points.at[i], load_sem.at[i]))
    fields = []
    for i, (source, target) in enumerate(((params_hbm, params), (side_hbm, side), (prior_hbm, prior))):
        for c in range(2):
            fields.append(
                pltpu.make_async_copy(
                    source.at[pl.ds(10 * c, 10), 0, :], target.at[pl.ds(16 * c, 10), :], field_sem.at[2 * i + c]
                )
            )
    for target in (params, side, prior):
        for c in range(2):
            target[16 * c + 8 : 16 * c + 16, :] = jnp.zeros((8, TILES), F32)
    for copy in fields + loads:
        copy.start()

    def send(source, target, send_sem, recv_sem, peer):
        copy = pltpu.make_async_remote_copy(
            src_ref=source, dst_ref=target, send_sem=send_sem, recv_sem=recv_sem, device_id=peer, device_id_type=MESH
        )
        copy.start()
        return copy

    def send_halo(source, turn):
        return [
            send(source, halo_in.at[turn, i], halo_send.at[turn, i], halo_recv.at[turn, i], borrowers[i])
            for i in range(4)
        ]

    def send_fold(turn):
        return [
            send(fold_out.at[turn, i], fold_in.at[turn, i], fold_send.at[turn, i], fold_recv.at[turn, i], owners[i])
            for i in range(4)
        ]

    for copy in fields:
        copy.wait()
    pl.semaphore_wait(barrier, 6 + len(line) + len(plane))
    halo = send_halo(params, 0)
    borders = [
        send(lists_ref, lists_in.at[0], list_send.at[0], list_recv.at[0], borrowers[2]),
        send(lists_ref, lists_in.at[1], list_send.at[1], list_recv.at[1], borrowers[3]),
    ]

    r = lax.broadcasted_iota(jnp.int32, (4 * LANES, 4 * LANES), 0)
    s = lax.broadcasted_iota(jnp.int32, (4 * LANES, 4 * LANES), 1)
    sort = jnp.where(r == 4 * lax.rem(s, LANES) + s // LANES, 1.0, 0.0).astype(BF16)
    slot = lax.broadcasted_iota(jnp.int32, (slots, LANES), 0)
    for copy in loads:
        copy.wait()

    @pl.loop(0, chunks)
    def _(tile):
        count = count_ref[tile]
        turned = lax.dot_general(
            points[tile].reshape(4 * LANES, slots), sort, (((0,), (0,)), ((), ())), preferred_element_type=F32
        )
        live = slot < count
        for c in range(4):
            coords[c] = jnp.where(live, turned[:, c * LANES : (c + 1) * LANES], 0.0)
        gram_tile(coords, gram, tile, count.astype(F32), slots)

    for copy in borders:
        copy.wait()
    second = second_ref[...]
    width = lists_ref.shape[1]
    index = jnp.where(second < 3 * TILES, second, -1).astype(F32)
    for i in range(2):
        start = 3 * TILES + i * width
        spot = lax.broadcasted_iota(jnp.int32, (width, pairs), 0) + start
        named = jnp.where(spot == second, 1.0, 0.0).astype(BF16)
        tile_at = matmul((lists_in[i] + 1).astype(F32).astype(BF16), named)[1 - i : 2 - i]
        index = jnp.where(tile_at > 0, tile_at + float((3 + i) * TILES - 1), index)
    index = index.astype(jnp.int32)
    column = lax.broadcasted_iota(jnp.int32, (TILES, pairs), 0)
    own_hot[...] = jnp.where(column == first_ref[...], 1.0, 0.0).astype(BF16)
    for i in range(5):
        other_hot[i * TILES : (i + 1) * TILES, :] = jnp.where(column + i * TILES == index, -1.0, 0.0).astype(BF16)

    def gathered(field, turn, halo):
        mine = thirds(field)
        own = joined(matmul(mine, own_hot[...]))
        other = matmul(mine, other_hot[:TILES, :])
        for copy in halo:
            copy.wait()
        others = jnp.concatenate([thirds(halo_in[turn, i]) for i in range(4)], axis=1)
        other = joined(other + matmul(others, other_hot[TILES:, :]))
        z_ref[0] = own
        z_ref[1] = other

    scale = 2.0 / slots

    def products():
        own, other = ([], []), ([], [])
        for tile in range(chunks):
            at = slice(tile * LANES, (tile + 1) * LANES)
            totals = [None, None]
            for n in range(20):
                block = gram[tile, n]
                for c in range(2):
                    row = 16 * c + n % 10
                    term = block * z_ref[n // 10, row : row + 1, at]
                    totals[c] = term if totals[c] is None else totals[c] + term
            for c in range(2):
                own[c].append(totals[c][:16] * scale)
                other[c].append(totals[c][16:] * scale)
        return tuple(
            jnp.concatenate([jnp.concatenate(half[c], axis=1) for c in range(2)], axis=0) for half in (own, other)
        )

    def scattered(own, other, turn):
        others = thirds(other)
        lent = joined(matmul_t(others, other_hot[TILES:, :]))
        for i in range(4):
            fold_out[turn, i] = lent[:, i * TILES : (i + 1) * TILES]
        fold = send_fold(turn)
        local = joined(matmul_t(thirds(own), own_hot[...]) + matmul_t(others, other_hot[:TILES, :]))
        return fold, local

    def folded(fold, local, turn):
        for copy in fold:
            copy.wait()
        return local + fold_in[turn, 0] + fold_in[turn, 1] + fold_in[turn, 2] + fold_in[turn, 3]

    start = params[...]
    gathered(start, 0, halo)
    own, other = products()
    fold, local = scattered(own, other, 0)
    local = local + prior[...] * start
    residual = side[...] - folded(fold, local, 0)

    direction[...] = residual
    halo = send_halo(direction, 1)
    squares = jnp.sum(residual * residual, keepdims=True)
    damped = prior[...] * residual
    gathered(residual, 1, halo)
    own, other = products()
    energy = jnp.sum(own * z_ref[0] + other * z_ref[1], keepdims=True) + jnp.sum(damped * residual, keepdims=True)
    lane = lax.broadcasted_iota(jnp.int32, (1, LANES), 1)
    total = jnp.where(lane < LANES // 2, squares, energy)
    part[0, 0:1, :] = total

    def send_part(turn, peers):
        return [
            send(
                part.at[turn, pl.ds(0, 1), :], part_in.at[turn, pl.ds(j, 1), :],
                part_send.at[turn, j], part_recv.at[turn, j], peer,
            )
            for j, peer in enumerate(peers)
        ]

    sums = send_part(0, line)
    fold, local = scattered(own, other, 1)
    local = local + damped
    for copy in sums:
        copy.wait()
    total = total + jnp.sum(part_in[0, : len(line), :], axis=0, keepdims=True)
    part[1, 0:1, :] = total
    sums = send_part(1, plane)
    image = folded(fold, local, 1)
    for copy in sums:
        copy.wait()
    total = total + jnp.sum(part_in[1, : len(plane), :], axis=0, keepdims=True)
    alpha = total[:, 0:1] / total[:, LANES // 2 : LANES // 2 + 1]
    answer = start + alpha * residual
    left = residual - alpha * image
    for c in range(2):
        for value, target in ((answer, solution_ref), (left, residual_ref)):
            target[10 * c : 10 * c + 10, :] = value[16 * c : 16 * c + 10]


def on_device(sizes, start_params, right_side, prior, matches, pair_first, pair_second, match_counts, send_lists):
    pairs, slots = matches.shape[2], matches.shape[4]
    width = send_lists.shape[3]
    secs, regs, group = sizes
    part_rows = -(-max(group, secs // group * regs) // 8) * 8
    chunks = pairs // LANES
    vmem = pl.BlockSpec(memory_space=pltpu.VMEM)
    hbm = pl.BlockSpec(memory_space=pl.ANY)
    field = (FIELD, TILES)
    dma = pltpu.SemaphoreType.DMA
    answer, left = pl.pallas_call(
        functools.partial(kernel, sizes),
        out_shape=(jax.ShapeDtypeStruct((20, TILES), F32),) * 2,
        in_specs=[hbm, hbm, hbm, hbm, vmem, vmem, vmem, vmem],
        out_specs=(vmem, vmem),
        scratch_shapes=[
            pltpu.VMEM(field, F32),
            pltpu.VMEM(field, F32),
            pltpu.VMEM(field, F32),
            pltpu.VMEM((chunks, LANES, 4, slots), BF16),
            pltpu.VMEM((4, slots, LANES), F32),
            pltpu.VMEM((chunks, 20, FIELD, LANES), F32),
            pltpu.VMEM((TILES, pairs), BF16),
            pltpu.VMEM((5 * TILES, pairs), BF16),
            pltpu.VMEM((2, FIELD, pairs), F32),
            pltpu.VMEM(field, F32),
            pltpu.VMEM((2, 2, width), jnp.int32),
            pltpu.VMEM((2, 4, *field), F32),
            pltpu.VMEM((2, 4, *field), F32),
            pltpu.VMEM((2, 4, *field), F32),
            pltpu.VMEM((2, 8, LANES), F32),
            pltpu.VMEM((2, part_rows, LANES), F32),
            dma((chunks,)),
            dma((6,)),
            dma((2,)),
            dma((2,)),
            dma((2, 4)),
            dma((2, 4)),
            dma((2, 4)),
            dma((2, 4)),
            dma((2, part_rows)),
            dma((2, part_rows)),
        ],
        compiler_params=pltpu.CompilerParams(collective_id=0, has_side_effects=True, vmem_limit_bytes=40 * 2**20),
    )(
        start_params.reshape(20, 1, TILES),
        right_side.reshape(20, 1, TILES),
        prior.reshape(20, 1, TILES),
        matches.reshape(pairs, 4, slots),
        pair_first.reshape(1, pairs),
        pair_second.reshape(1, pairs),
        match_counts.reshape(chunks, 1, LANES),
        send_lists.reshape(2, width),
    )
    return answer[None, None], left[None, None]


def solution(mesh):
    secs, regs = mesh.shape["sec"], mesh.shape["reg"]
    group = 16 if secs % 16 == 0 else secs
    wide = P("sec", "reg", None, None)
    return jax.shard_map(
        functools.partial(on_device, (secs, regs, group)),
        mesh=mesh,
        in_specs=(
            wide, wide, wide, P("sec", "reg", None, None, None),
            P("sec", "reg", None), P("sec", "reg", None), P("sec", "reg", None), wide,
        ),
        out_specs=(wide, wide),
        check_vma=False,
    )
```

time: 506 us -> 47 us (0.09); the launches traced: 497 us -> 46.6 us
  local copies, waits for them, and re-layouts: 185 us -> 7.36 us
  matrix products: 93.3 us -> 0 us
  blocking collectives: 84.8 us -> 0 us
  other arithmetic: 74.4 us -> 0 us
  starting transfers between devices: 42.1 us -> 0 us
  Pallas kernels: 0 us -> 38.6 us
  waiting for transfers between devices: 14.2 us -> 0 us
    another operation x36 -> x0, local copies, waits for them, and re-layouts: 106 us -> none  [the longest x20 102 us: monomials(): jnp.stack([constant, across, upward, square_a, mixed, square_b, square_a...]
    dot_general x40 -> x0, matrix products: 93.3 us -> none  [the longest x10 34.1 us: block_terms(): jnp.einsum('mpk,cpk->cmp', basis_a, mismatch, precision=FULL_PRECISION)]
    psum x1 -> x0, blocking collectives: 84.8 us -> none  [global_dot(): return lax.psum(value, ('sec', 'reg'))]
    ppermute x16 -> x0, starting transfers between devices: 42.1 us -> none  [the longest x8 23.6 us: shifted(): return lax.ppermute(array, axis, pairs)]
    pallas_call x0 -> x1, Pallas kernels: none -> 38.6 us  [on_device(): pl.pallas_call(functools.partial(kernel, sizes), out_shape=(jax.ShapeDtyp...]
    gather x24 -> x0, local copies, waits for them, and re-layouts: 33.9 us -> none  [the longest x10 15.8 us: block_terms(): other = jnp.take(extended, second_blk, axis=1).reshape(2, 10, width)]
    scatter-add x8 -> x0, other arithmetic: 28.1 us -> none  [the longest x4 25 us: apply_normal(): products = products.at[:, first].add(to_own).at[:, second].add(to_other)]
    mul x20 -> x0, other arithmetic: 27 us -> none  [the longest x10 19.2 us: monomials(): square_b * upward]
  transfers between devices with their start and end apart: 16 -> 0, of which waited for: 5 -> 0; matrix products, arithmetic and copies ran while one was open for 2% -> 0% of each run, Pallas kernels for 0% -> 0%
where the time goes in v1:
time: 47 us; the launch traced here: 46.6 us
  Pallas kernels  38.6 us (82%)
  local copies, waits for them, and re-layouts  7.36 us (16%)
  between operations  0.66 us (1%)
    pallas_call x1, Pallas kernels, on_device(): pl.pallas_call(functools.partial(kernel, sizes), out_shape=(jax.ShapeDtyp...  38.6 us
    unnamed x18, local copies, waits for them, and re-layouts  7.36 us

profile of v1, /device:TPU:1, one launch (start us, length us, event | category | flops | bytes accessed | tf_op | source)
XLA Modules:
  0.0 46.6 jit_solution(16049285145137083589)
XLA Ops:
  0.6 0.0 copy-start
  0.6 1.3 %copy-done = bf16[1,1,640,4,256]{4,3,2,1,0:T(4,128)(2,1)S(1)} copy-done((bf16[1,1,640,4,256]{4,3,2,1,0:T(4,128)(2,1)S(1)}, bf16[1,1,640,4,256]{4,3,2,1,0:T(4,128)(2,1)}, u32[]{:S(2)}) %copy-start) | copy-done | bytes 1310744
  1.9 0.0 copy-start.1
  2.0 0.7 %copy-done.1 = f32[1,1,20,128]{3,1,2,0:T(1,128)S(1)} copy-done((f32[1,1,20,128]{3,1,2,0:T(1,128)S(1)}, f32[1,1,20,128]{3,1,2,0:T(1,128)}, u32[]{:S(2)}) %copy-start.1) | copy-done | bytes 10264
  2.7 0.0 copy-start.2
  2.7 0.7 %copy-done.2 = f32[1,1,20,128]{3,1,2,0:T(1,128)S(1)} copy-done((f32[1,1,20,128]{3,1,2,0:T(1,128)S(1)}, f32[1,1,20,128]{3,1,2,0:T(1,128)}, u32[]{:S(2)}) %copy-start.2) | copy-done | bytes 10264
  3.4 0.0 copy-start.3
  3.4 0.7 %copy-done.3 = f32[1,1,20,128]{3,1,2,0:T(1,128)S(1)} copy-done((f32[1,1,20,128]{3,1,2,0:T(1,128)S(1)}, f32[1,1,20,128]{3,1,2,0:T(1,128)}, u32[]{:S(2)}) %copy-start.3) | copy-done | bytes 10264
  4.1 0.0 copy-start.4
  4.1 0.7 %copy-done.4 = s32[1,1,640]{2,1,0:T(1,128)S(1)} copy-done((s32[1,1,640]{2,1,0:T(1,128)S(1)}, s32[1,1,640]{2,1,0:T(1,128)}, u32[]{:S(2)}) %copy-start.4) | copy-done | bytes 2584
  4.7 0.0 copy-start.5
  4.7 0.7 %copy-done.5 = s32[1,1,640]{2,1,0:T(1,128)S(1)} copy-done((s32[1,1,640]{2,1,0:T(1,128)S(1)}, s32[1,1,640]{2,1,0:T(1,128)}, u32[]{:S(2)}) %copy-start.5) | copy-done | bytes 2584
  5.4 0.0 copy-start.6
  5.4 0.7 %copy-done.6 = s32[1,1,640]{2,1,0:T(1,128)S(1)} copy-done((s32[1,1,640]{2,1,0:T(1,128)S(1)}, s32[1,1,640]{2,1,0:T(1,128)}, u32[]{:S(2)}) %copy-start.6) | copy-done | bytes 2584
  6.1 0.0 copy-start.7
  6.1 0.7 %copy-done.7 = s32[1,1,2,16]{3,2,1,0:T(2,128)S(1)} copy-done((s32[1,1,2,16]{3,2,1,0:T(2,128)S(1)}, s32[1,1,2,16]{3,2,1,0:T(2,128)}, u32[]{:S(2)}) %copy-start.7) | copy-done | bytes 152
  6.8 38.6 %shard_map.95 = (f32[20,128]{1,0:T(8,128)S(1)}, f32[20,128]{1,0:T(8,128)S(1)}) custom-call(f32[20,1,128]{2,1,0:T(1,128)S(1)} %bitcast.13, f32[20,1,128]{2,1,0:T(1,128)S(1)} %bitcast.14, f32[20,1,128]{2,1,0:T(1,128)S(1)} %bitcast.15, bf16[640,4,256]{2,1,0:T(4,128)(2,1)S(1)} %bitcast.10, s32[1,640]{1,0:T(1,128)S(1)} %bitcast.16, s32[1,640]{1,0:T(1,128)S(1)} %bitcast.17, ...), custom_call_target="tpu_custom_call" | custom-call | tf_op jit(solution)/shard_map/pallas_call | solution.py:322
  45.4 0.6 %copy.10 = f32[1,1,20,128]{3,1,2,0:T(1,128)} copy(f32[1,1,20,128]{3,2,1,0:T(8,128)S(1)} %bitcast.12) | data formatting | bytes 20480
  46.0 0.6 %copy.11 = f32[1,1,20,128]{3,1,2,0:T(1,128)} copy(f32[1,1,20,128]{3,2,1,0:T(8,128)S(1)} %bitcast.11) | data formatting | bytes 20480
Async XLA Ops:
  0.6 1.3 %copy-start = (bf16[1,1,640,4,256]{4,3,2,1,0:T(4,128)(2,1)S(1)}, bf16[1,1,640,4,256]{4,3,2,1,0:T(4,128)(2,1)}, u32[]{:S(2)}) copy-start(bf16[1,1,640,4,256]{4,3,2,1,0:T(4,128)(2,1)} %param.11) | copy-start | bytes 3932164
  1.9 0.7 %copy-start.1 = (f32[1,1,20,128]{3,1,2,0:T(1,128)S(1)}, f32[1,1,20,128]{3,1,2,0:T(1,128)}, u32[]{:S(2)}) copy-start(f32[1,1,20,128]{3,1,2,0:T(1,128)} %param.8) | copy-start | bytes 30724
  2.7 0.7 %copy-start.2 = (f32[1,1,20,128]{3,1,2,0:T(1,128)S(1)}, f32[1,1,20,128]{3,1,2,0:T(1,128)}, u32[]{:S(2)}) copy-start(f32[1,1,20,128]{3,1,2,0:T(1,128)} %param.9) | copy-start | bytes 30724
  3.4 0.7 %copy-start.3 = (f32[1,1,20,128]{3,1,2,0:T(1,128)S(1)}, f32[1,1,20,128]{3,1,2,0:T(1,128)}, u32[]{:S(2)}) copy-start(f32[1,1,20,128]{3,1,2,0:T(1,128)} %param.10) | copy-start | bytes 30724
  4.1 0.7 %copy-start.4 = (s32[1,1,640]{2,1,0:T(1,128)S(1)}, s32[1,1,640]{2,1,0:T(1,128)}, u32[]{:S(2)}) copy-start(s32[1,1,640]{2,1,0:T(1,128)} %param.12) | copy-start | bytes 7684
  4.7 0.7 %copy-start.5 = (s32[1,1,640]{2,1,0:T(1,128)S(1)}, s32[1,1,640]{2,1,0:T(1,128)}, u32[]{:S(2)}) copy-start(s32[1,1,640]{2,1,0:T(1,128)} %param.13) | copy-start | bytes 7684
  5.4 0.7 %copy-start.6 = (s32[1,1,640]{2,1,0:T(1,128)S(1)}, s32[1,1,640]{2,1,0:T(1,128)}, u32[]{:S(2)}) copy-start(s32[1,1,640]{2,1,0:T(1,128)} %param.14) | copy-start | bytes 7684
  6.1 0.7 %copy-start.7 = (s32[1,1,2,16]{3,2,1,0:T(2,128)S(1)}, s32[1,1,2,16]{3,2,1,0:T(2,128)}, u32[]{:S(2)}) copy-start(s32[1,1,2,16]{3,2,1,0:T(2,128)} %param.15) | copy-start | bytes 388

commit v2 on v1

--- a/solution.py
+++ b/solution.py
@@ -14,7 +14,8 @@
 TILES = 128
 LANES = 128
 FIELD = 32
-UNROLL = 8
+UNROLL = 16
+EARLY = 2
 
 
 def powers(x, y):
@@ -106,15 +107,15 @@
 
 
 def kernel(
-    sizes, params_hbm, side_hbm, prior_hbm, matches_hbm, first_ref, second_ref, count_ref, lists_ref,
+    sizes, params_hbm, side_hbm, prior_hbm, matches_hbm, first_hbm, second_hbm, count_hbm, lists_hbm,
     solution_ref, residual_ref,
-    params, side, prior, points, coords, gram, own_hot, other_hot, z_ref,
+    first_ref, second_ref, count_ref, lists_ref, params, side, prior, points, coords, gram, own_hot, other_hot, z_ref,
     direction, lists_in, halo_in, fold_out, fold_in, part, part_in,
-    load_sem, field_sem, list_send, list_recv, halo_send, halo_recv, fold_send, fold_recv, part_send, part_recv,
+    load_sem, small_sem, field_sem, list_send, list_recv, halo_send, halo_recv, fold_send, fold_recv, part_send, part_recv,
 ):
     secs, regs, group = sizes
     sec, reg = lax.axis_index("sec"), lax.axis_index("reg")
-    pairs = first_ref.shape[1]
+    pairs = first_hbm.shape[1]
     slots = matches_hbm.shape[2]
     chunks = pairs // LANES
     rows = secs // group
@@ -151,14 +152,23 @@
     for target in (params, side, prior):
         for c in range(2):
             target[16 * c + 8 : 16 * c + 16, :] = jnp.zeros((8, TILES), F32)
-    for copy in fields + loads:
+    small = [
+        pltpu.make_async_copy(source, target, small_sem.at[i])
+        for i, (source, target) in enumerate(
+            ((lists_hbm, lists_ref), (count_hbm, count_ref), (first_hbm, first_ref), (second_hbm, second_ref))
+        )
+    ]
+    for copy in fields[:2] + small[:1] + loads[:1] + small[1:2] + loads[1:] + small[2:] + fields[2:]:
         copy.start()
+
+    sent = []
 
     def send(source, target, send_sem, recv_sem, peer):
         copy = pltpu.make_async_remote_copy(
             src_ref=source, dst_ref=target, send_sem=send_sem, recv_sem=recv_sem, device_id=peer, device_id_type=MESH
         )
         copy.start()
+        sent.append(copy)
         return copy
 
     def send_halo(source, turn):
@@ -173,24 +183,12 @@
             for i in range(4)
         ]
 
-    for copy in fields:
-        copy.wait()
-    pl.semaphore_wait(barrier, 6 + len(line) + len(plane))
-    halo = send_halo(params, 0)
-    borders = [
-        send(lists_ref, lists_in.at[0], list_send.at[0], list_recv.at[0], borrowers[2]),
-        send(lists_ref, lists_in.at[1], list_send.at[1], list_recv.at[1], borrowers[3]),
-    ]
-
     r = lax.broadcasted_iota(jnp.int32, (4 * LANES, 4 * LANES), 0)
     s = lax.broadcasted_iota(jnp.int32, (4 * LANES, 4 * LANES), 1)
     sort = jnp.where(r == 4 * lax.rem(s, LANES) + s // LANES, 1.0, 0.0).astype(BF16)
     slot = lax.broadcasted_iota(jnp.int32, (slots, LANES), 0)
-    for copy in loads:
-        copy.wait()
-
-    @pl.loop(0, chunks)
-    def _(tile):
+
+    def form(tile):
         count = count_ref[tile]
         turned = lax.dot_general(
             points[tile].reshape(4 * LANES, slots), sort, (((0,), (0,)), ((), ())), preferred_element_type=F32
@@ -200,8 +198,23 @@
             coords[c] = jnp.where(live, turned[:, c * LANES : (c + 1) * LANES], 0.0)
         gram_tile(coords, gram, tile, count.astype(F32), slots)
 
+    for copy in small[1:] + fields[2:] + loads:
+        copy.wait()
+    pl.loop(0, EARLY)(form)
+    for copy in fields[:2] + small[:1]:
+        copy.wait()
+    pl.semaphore_wait(barrier, 6 + len(line) + len(plane))
+    halo = send_halo(params, 0)
+    borders = [
+        send(lists_ref, lists_in.at[0], list_send.at[0], list_recv.at[0], borrowers[2]),
+        send(lists_ref, lists_in.at[1], list_send.at[1], list_recv.at[1], borrowers[3]),
+    ]
+
+
+    pl.loop(EARLY, chunks)(form)
+
     for copy in borders:
-        copy.wait()
+        copy.wait_recv()
     second = second_ref[...]
     width = lists_ref.shape[1]
     index = jnp.where(second < 3 * TILES, second, -1).astype(F32)
@@ -222,7 +235,7 @@
         own = joined(matmul(mine, own_hot[...]))
         other = matmul(mine, other_hot[:TILES, :])
         for copy in halo:
-            copy.wait()
+            copy.wait_recv()
         others = jnp.concatenate([thirds(halo_in[turn, i]) for i in range(4)], axis=1)
         other = joined(other + matmul(others, other_hot[TILES:, :]))
         z_ref[0] = own
@@ -259,7 +272,7 @@
 
     def folded(fold, local, turn):
         for copy in fold:
-            copy.wait()
+            copy.wait_recv()
         return local + fold_in[turn, 0] + fold_in[turn, 1] + fold_in[turn, 2] + fold_in[turn, 3]
 
     start = params[...]
@@ -293,15 +306,17 @@
     fold, local = scattered(own, other, 1)
     local = local + damped
     for copy in sums:
-        copy.wait()
+        copy.wait_recv()
     total = total + jnp.sum(part_in[0, : len(line), :], axis=0, keepdims=True)
     part[1, 0:1, :] = total
     sums = send_part(1, plane)
     image = folded(fold, local, 1)
     for copy in sums:
-        copy.wait()
+        copy.wait_recv()
     total = total + jnp.sum(part_in[1, : len(plane), :], axis=0, keepdims=True)
     alpha = total[:, 0:1] / total[:, LANES // 2 : LANES // 2 + 1]
+    for copy in sent:
+        copy.wait_send()
     answer = start + alpha * residual
     left = residual - alpha * image
     for c in range(2):
@@ -316,15 +331,19 @@
     part_rows = -(-max(group, secs // group * regs) // 8) * 8
     chunks = pairs // LANES
     vmem = pl.BlockSpec(memory_space=pltpu.VMEM)
-    hbm = pl.BlockSpec(memory_space=pl.ANY)
+    hbm = pl.BlockSpec(memory_space=pltpu.HBM)
     field = (FIELD, TILES)
     dma = pltpu.SemaphoreType.DMA
     answer, left = pl.pallas_call(
         functools.partial(kernel, sizes),
         out_shape=(jax.ShapeDtypeStruct((20, TILES), F32),) * 2,
-        in_specs=[hbm, hbm, hbm, hbm, vmem, vmem, vmem, vmem],
+        in_specs=[hbm] * 8,
         out_specs=(vmem, vmem),
         scratch_shapes=[
+            pltpu.VMEM((1, pairs), jnp.int32),
+            pltpu.VMEM((1, pairs), jnp.int32),
+            pltpu.VMEM((chunks, 1, LANES), jnp.int32),
+            pltpu.VMEM((2, width), jnp.int32),
             pltpu.VMEM(field, F32),
             pltpu.VMEM(field, F32),
             pltpu.VMEM(field, F32),
@@ -342,6 +361,7 @@
             pltpu.VMEM((2, 8, LANES), F32),
             pltpu.VMEM((2, part_rows, LANES), F32),
             dma((chunks,)),
+            dma((4,)),
             dma((6,)),
             dma((2,)),
             dma((2,)),
@@ -352,8 +372,8 @@
             dma((2, part_rows)),
             dma((2, part_rows)),
         ],
-        compiler_params=pltpu.CompilerParams(collective_id=0, has_side_effects=True, vmem_limit_bytes=40 * 2**20),
-    )(
+        compiler_params=pltpu.CompilerParams(collective_id=0, has_side_effects=True, vmem_limit_bytes=32 * 2**20),
+    )(*[pltpu.with_memory_space_constraint(x, pltpu.HBM) for x in (
         start_params.reshape(20, 1, TILES),
         right_side.reshape(20, 1, TILES),
         prior.reshape(20, 1, TILES),
@@ -362,7 +382,7 @@
         pair_second.reshape(1, pairs),
         match_counts.reshape(chunks, 1, LANES),
         send_lists.reshape(2, width),
-    )
+    )])
     return answer[None, None], left[None, None]
 
 

time: 47 us -> 40.2 us (0.86)
  local copies, waits for them, and re-layouts: 7.36 us -> 1.22 us
    unnamed x18 -> x2, local copies, waits for them, and re-layouts: 7.36 us -> 1.22 us
where the time goes in v2:
time: 40.2 us; the launch traced here: 40.1 us
  Pallas kernels  38.2 us (95%)
  local copies, waits for them, and re-layouts  1.22 us (3%)
  between operations  0.64 us (2%)
    pallas_call x1, Pallas kernels, on_device(): pl.pallas_call(functools.partial(kernel, sizes), out_shape=(jax.ShapeDtyp...  38.2 us
    unnamed x2, local copies, waits for them, and re-layouts  1.22 us

profile of v2, /device:TPU:1, one launch (start us, length us, event | category | flops | bytes accessed | tf_op | source)
XLA Modules:
  0.0 40.1 jit_solution(9923141486241854580)
XLA Ops:
  0.6 38.2 %shard_map.95 = (f32[20,128]{1,0:T(8,128)S(1)}, f32[20,128]{1,0:T(8,128)S(1)}) custom-call(f32[20,1,128]{2,1,0:T(1,128)} %bitcast.13, f32[20,1,128]{2,1,0:T(1,128)} %bitcast.14, f32[20,1,128]{2,1,0:T(1,128)} %bitcast.15, bf16[640,4,256]{2,1,0:T(4,128)(2,1)} %bitcast.12, s32[1,640]{1,0:T(1,128)} %bitcast.16, s32[1,640]{1,0:T(1,128)} %bitcast.17, ...), custom_call_target="tpu_custom_call" | custom-call | tf_op jit(solution)/shard_map/pallas_call | solution.py:337
  38.9 0.6 %copy.10 = f32[1,1,20,128]{3,1,2,0:T(1,128)} copy(f32[1,1,20,128]{3,2,1,0:T(8,128)S(1)} %bitcast.11) | data formatting | bytes 20480
  39.5 0.6 %copy.11 = f32[1,1,20,128]{3,1,2,0:T(1,128)} copy(f32[1,1,20,128]{3,2,1,0:T(8,128)S(1)} %bitcast.10) | data formatting | bytes 20480

commit v3 on v2

--- a/solution.py
+++ b/solution.py
@@ -15,7 +15,9 @@
 LANES = 128
 FIELD = 32
 UNROLL = 16
-EARLY = 2
+EARLY = 1
+FORMED = 3
+GROUPS = ((1, 2, 3), (4, 5, 6), (7, 8, 9))
 
 
 def powers(x, y):
@@ -37,12 +39,12 @@
     return 16 * (n // 10) + n % 10
 
 
-def gram_tile(coords, gram, tile, count, slots):
+def gram_tile(coords, gram, tile, valid, slots):
     zero = jnp.zeros((8, LANES), F32)
     gram[tile, :, 8:16, :] = jnp.zeros((20, 8, LANES), F32)
     gram[tile, :, 24:32, :] = jnp.zeros((20, 8, LANES), F32)
 
-    def sums(terms, which):
+    def sums(terms, which, count):
         def step(i, totals):
             for u in range(UNROLL):
                 at = pl.multiple_of((i * UNROLL + u) * 8, 8)
@@ -50,7 +52,8 @@
                 totals = tuple(a + b for a, b in zip(totals, new))
             return totals
 
-        totals = lax.fori_loop(0, slots // 8 // UNROLL, step, (zero,) * 27)
+        trips = slots // 8 // UNROLL
+        totals = step(0, (zero,) * count) if trips == 1 else lax.fori_loop(0, trips, step, (zero,) * count)
         return [jnp.sum(t, axis=0, keepdims=True) for t in totals]
 
     def put(n, m, row):
@@ -58,8 +61,8 @@
         gram[tile, n, r : r + 1, :] = row
 
     for side in range(2):
-        table = dict(zip(MOMENTS, sums(moments, (2 * side, 2 * side + 1))))
-        table[0, 0] = count
+        table = dict(zip(MOMENTS, sums(moments, (2 * side, 2 * side + 1), 27)))
+        table[0, 0] = valid
         for n, (i, j) in enumerate(EXPONENTS):
             for m, (k, l) in enumerate(EXPONENTS):
                 put(10 * side + n, 10 * side + m, table[i + k, j + l])
@@ -70,14 +73,13 @@
             elif n:
                 put(10, n, table[e])
                 put(n, 10, table[e])
-    for group in range(3):
-        some = range(1 + 3 * group, 4 + 3 * group)
+    for some in GROUPS:
 
         def terms(xa, ya, xb, yb):
             a, b = powers(xa, ya), powers(xb, yb)
             return [a[m] * b[n] for m in some for n in range(1, 10)]
 
-        rows = iter(sums(terms, (0, 1, 2, 3)))
+        rows = iter(sums(terms, (0, 1, 2, 3), 9 * len(some)))
         for m in some:
             for n in range(1, 10):
                 row = next(rows)
@@ -109,8 +111,8 @@
 def kernel(
     sizes, params_hbm, side_hbm, prior_hbm, matches_hbm, first_hbm, second_hbm, count_hbm, lists_hbm,
     solution_ref, residual_ref,
-    first_ref, second_ref, count_ref, lists_ref, params, side, prior, points, coords, gram, own_hot, other_hot, z_ref,
-    direction, lists_in, halo_in, fold_out, fold_in, part, part_in,
+    first_ref, second_ref, count_ref, lists_ref, params, side, prior, points, coords, sort_ref, gram, own_hot, other_hot, z_ref,
+    y_ref, direction, lists_in, halo_in, fold_out, fold_in, part, part_in,
     load_sem, small_sem, field_sem, list_send, list_recv, halo_send, halo_recv, fold_send, fold_recv, part_send, part_recv,
 ):
     secs, regs, group = sizes
@@ -119,7 +121,6 @@
     slots = matches_hbm.shape[2]
     chunks = pairs // LANES
     rows = secs // group
-    part_count = rows * regs
 
     def device(by_sec, by_reg):
         return (lax.rem(sec + by_sec + secs, secs), lax.rem(reg + by_reg + regs, regs))
@@ -127,16 +128,11 @@
     borrowers = [device(1, 0), device(2, 0), device(0, 1), device(0, -1)]
     owners = [device(-1, 0), device(-2, 0), device(0, -1), device(0, 1)]
     base, place = group * (sec // group), lax.rem(sec, group)
-    line = [(base + lax.rem(place + j, group), reg) for j in range(1, group)]
-    here = (sec // group) * regs + reg
-    plane = []
-    for j in range(1, part_count):
-        there = lax.rem(here + j, part_count)
-        plane.append(((there // regs) * group + place, lax.rem(there, regs)))
-
-    barrier = pltpu.get_barrier_semaphore()
-    for peer in borrowers + owners[:2] + line + plane:
-        pl.semaphore_signal(barrier, inc=1, device_id=peer, device_id_type=MESH)
+    line = [(base + lax.rem(place + j, group), reg) for j in sorted(range(1, group), key=lambda j: abs(2 * j - group))]
+    hops = [(min(a, rows - a) + min(b, regs - b), a, b) for a in range(rows) for b in range(regs) if a or b]
+    plane = [
+        (lax.rem(sec // group + a, rows) * group + place, lax.rem(reg + b, regs)) for _, a, b in sorted(hops, reverse=True)
+    ]
 
     loads = []
     for i in range(chunks):
@@ -151,7 +147,7 @@
             )
     for target in (params, side, prior):
         for c in range(2):
-            target[16 * c + 8 : 16 * c + 16, :] = jnp.zeros((8, TILES), F32)
+            target[16 * c + 10 : 16 * c + 16, :] = jnp.zeros((6, TILES), F32)
     small = [
         pltpu.make_async_copy(source, target, small_sem.at[i])
         for i, (source, target) in enumerate(
@@ -161,6 +157,10 @@
     for copy in fields[:2] + small[:1] + loads[:1] + small[1:2] + loads[1:] + small[2:] + fields[2:]:
         copy.start()
 
+    barrier = pltpu.get_barrier_semaphore()
+    for peer in borrowers + owners[:2] + line + plane:
+        pl.semaphore_signal(barrier, inc=1, device_id=peer, device_id_type=MESH)
+
     sent = []
 
     def send(source, target, send_sem, recv_sem, peer):
@@ -185,18 +185,25 @@
 
     r = lax.broadcasted_iota(jnp.int32, (4 * LANES, 4 * LANES), 0)
     s = lax.broadcasted_iota(jnp.int32, (4 * LANES, 4 * LANES), 1)
-    sort = jnp.where(r == 4 * lax.rem(s, LANES) + s // LANES, 1.0, 0.0).astype(BF16)
+    sort_ref[...] = jnp.where(r == 4 * lax.rem(s, LANES) + s // LANES, 1.0, 0.0).astype(BF16)
     slot = lax.broadcasted_iota(jnp.int32, (slots, LANES), 0)
 
+    def turn(tile, to):
+        turned = lax.dot_general(
+            points[tile].reshape(4 * LANES, slots), sort_ref[...], (((0,), (0,)), ((), ())), preferred_element_type=F32
+        )
+        live = slot < count_ref[tile]
+        for c in range(4):
+            coords[to, c] = jnp.where(live, turned[:, c * LANES : (c + 1) * LANES], 0.0)
+        coords[to, 4] = jnp.where(live, 1.0, 0.0)
+
+    def gram_of(tile, at):
+        gram_tile(coords.at[at], gram, tile, count_ref[tile].astype(F32), slots)
+
     def form(tile):
-        count = count_ref[tile]
-        turned = lax.dot_general(
-            points[tile].reshape(4 * LANES, slots), sort, (((0,), (0,)), ((), ())), preferred_element_type=F32
-        )
-        live = slot < count
-        for c in range(4):
-            coords[c] = jnp.where(live, turned[:, c * LANES : (c + 1) * LANES], 0.0)
-        gram_tile(coords, gram, tile, count.astype(F32), slots)
+        at = lax.rem(tile, 2)
+        turn(tile, at)
+        gram_of(tile, at)
 
     for copy in small[1:] + fields[2:] + loads:
         copy.wait()
@@ -211,7 +218,9 @@
     ]
 
 
-    pl.loop(EARLY, chunks)(form)
+    pl.loop(EARLY, FORMED)(form)
+    for tile in range(FORMED, chunks):
+        turn(tile, tile % 2)
 
     for copy in borders:
         copy.wait_recv()
@@ -243,9 +252,8 @@
 
     scale = 2.0 / slots
 
-    def products():
-        own, other = ([], []), ([], [])
-        for tile in range(chunks):
+    def products(tiles):
+        for tile in range(tiles):
             at = slice(tile * LANES, (tile + 1) * LANES)
             totals = [None, None]
             for n in range(20):
@@ -255,13 +263,38 @@
                     term = block * z_ref[n // 10, row : row + 1, at]
                     totals[c] = term if totals[c] is None else totals[c] + term
             for c in range(2):
-                own[c].append(totals[c][:16] * scale)
-                other[c].append(totals[c][16:] * scale)
-        return tuple(
-            jnp.concatenate([jnp.concatenate(half[c], axis=1) for c in range(2)], axis=0) for half in (own, other)
-        )
-
-    def scattered(own, other, turn):
+                for half in range(2):
+                    y_ref[half, 16 * c : 16 * c + 16, at] = totals[c][16 * half : 16 * half + 16]
+
+    def direct(tile):
+        at = slice(tile * LANES, (tile + 1) * LANES)
+        points_of = coords.at[tile % 2]
+        for c in range(2):
+            z = [[z_ref[half, 16 * c + m : 16 * c + m + 1, at] for m in range(10)] for half in range(2)]
+            constant = z[0][0] + z[1][0]
+
+            def step(i, totals):
+                for u in range(UNROLL):
+                    here = pl.multiple_of((i * UNROLL + u) * 8, 8)
+                    xa, ya, xb, yb, live = [points_of[d, pl.ds(here, 8), :] for d in range(5)]
+                    basis = powers(xa, ya)[1:] + powers(xb, yb)[1:]
+                    first_half, second_half = constant + z[0][1] * xa, z[1][1] * xb
+                    for m in range(1, 9):
+                        first_half = first_half + z[0][m + 1] * basis[m]
+                        second_half = second_half + z[1][m + 1] * basis[9 + m]
+                    mismatch = (first_half + second_half) * live
+                    totals = (totals[0] + mismatch,) + tuple(t + b * mismatch for t, b in zip(totals[1:], basis))
+                return totals
+
+            totals = lax.fori_loop(0, slots // 8 // UNROLL, step, (jnp.zeros((8, LANES), F32),) * 19)
+            totals = [jnp.sum(t, axis=0, keepdims=True) for t in totals]
+            for half in range(2):
+                y_ref[half, 16 * c : 16 * c + 1, at] = totals[0]
+                for m in range(1, 10):
+                    y_ref[half, 16 * c + m : 16 * c + m + 1, at] = totals[9 * half + m]
+
+    def scattered(turn):
+        own, other = y_ref[0] * scale, y_ref[1] * scale
         others = thirds(other)
         lent = joined(matmul_t(others, other_hot[TILES:, :]))
         for i in range(4):
@@ -277,18 +310,26 @@
 
     start = params[...]
     gathered(start, 0, halo)
-    own, other = products()
-    fold, local = scattered(own, other, 0)
+    for c in range(2):
+        for half in range(2):
+            y_ref[half, 16 * c + 10 : 16 * c + 16, :] = jnp.zeros((6, pairs), F32)
+    for tile in range(FORMED, chunks):
+        direct(tile)
+    products(FORMED)
+    fold, local = scattered(0)
+    for tile in range(FORMED, chunks - 1):
+        gram_of(tile, tile % 2)
     local = local + prior[...] * start
     residual = side[...] - folded(fold, local, 0)
 
     direction[...] = residual
     halo = send_halo(direction, 1)
+    gram_of(chunks - 1, (chunks - 1) % 2)
     squares = jnp.sum(residual * residual, keepdims=True)
     damped = prior[...] * residual
     gathered(residual, 1, halo)
-    own, other = products()
-    energy = jnp.sum(own * z_ref[0] + other * z_ref[1], keepdims=True) + jnp.sum(damped * residual, keepdims=True)
+    products(chunks)
+    energy = scale * jnp.sum(y_ref[0] * z_ref[0] + y_ref[1] * z_ref[1], keepdims=True) + jnp.sum(damped * residual, keepdims=True)
     lane = lax.broadcasted_iota(jnp.int32, (1, LANES), 1)
     total = jnp.where(lane < LANES // 2, squares, energy)
     part[0, 0:1, :] = total
@@ -303,7 +344,7 @@
         ]
 
     sums = send_part(0, line)
-    fold, local = scattered(own, other, 1)
+    fold, local = scattered(1)
     local = local + damped
     for copy in sums:
         copy.wait_recv()
@@ -348,10 +389,12 @@
             pltpu.VMEM(field, F32),
             pltpu.VMEM(field, F32),
             pltpu.VMEM((chunks, LANES, 4, slots), BF16),
-            pltpu.VMEM((4, slots, LANES), F32),
+            pltpu.VMEM((2, 5, slots, LANES), F32),
+            pltpu.VMEM((4 * LANES, 4 * LANES), BF16),
             pltpu.VMEM((chunks, 20, FIELD, LANES), F32),
             pltpu.VMEM((TILES, pairs), BF16),
             pltpu.VMEM((5 * TILES, pairs), BF16),
+            pltpu.VMEM((2, FIELD, pairs), F32),
             pltpu.VMEM((2, FIELD, pairs), F32),
             pltpu.VMEM(field, F32),
             pltpu.VMEM((2, 2, width), jnp.int32),

time: 40.2 us -> 37.7 us (0.938)
  Pallas kernels: 38.2 us -> 35.7 us
    pallas_call x1, Pallas kernels: 38.2 us -> 35.7 us  [on_device(): pl.pallas_call(functools.partial(kernel, sizes), out_shape=(jax.ShapeDtyp...]
where the time goes in v3:
time: 37.7 us; the launch traced here: 37.6 us
  Pallas kernels  35.7 us (95%)
  local copies, waits for them, and re-layouts  1.22 us (3%)
  between operations  0.64 us (2%)
    pallas_call x1, Pallas kernels, on_device(): pl.pallas_call(functools.partial(kernel, sizes), out_shape=(jax.ShapeDtyp...  35.7 us
    unnamed x2, local copies, waits for them, and re-layouts  1.22 us

profile of v3, /device:TPU:1, one launch (start us, length us, event | category | flops | bytes accessed | tf_op | source)
XLA Modules:
  0.0 37.6 jit_solution(3672895805015664695)
XLA Ops:
  0.6 35.7 %shard_map.95 = (f32[20,128]{1,0:T(8,128)S(1)}, f32[20,128]{1,0:T(8,128)S(1)}) custom-call(f32[20,1,128]{2,1,0:T(1,128)} %bitcast.13, f32[20,1,128]{2,1,0:T(1,128)} %bitcast.14, f32[20,1,128]{2,1,0:T(1,128)} %bitcast.15, bf16[640,4,256]{2,1,0:T(4,128)(2,1)} %bitcast.12, s32[1,640]{1,0:T(1,128)} %bitcast.16, s32[1,640]{1,0:T(1,128)} %bitcast.17, ...), custom_call_target="tpu_custom_call" | custom-call | tf_op jit(solution)/shard_map/pallas_call | solution.py:378
  36.4 0.6 %copy.10 = f32[1,1,20,128]{3,1,2,0:T(1,128)} copy(f32[1,1,20,128]{3,2,1,0:T(8,128)S(1)} %bitcast.11) | data formatting | bytes 20480
  37.0 0.6 %copy.11 = f32[1,1,20,128]{3,1,2,0:T(1,128)} copy(f32[1,1,20,128]{3,2,1,0:T(8,128)S(1)} %bitcast.10) | data formatting | bytes 20480

commit v4 on v3

--- a/solution.py
+++ b/solution.py
@@ -137,49 +137,58 @@
     loads = []
     for i in range(chunks):
         loads.append(pltpu.make_async_copy(matches_hbm.at[pl.ds(i * LANES, LANES)], points.at[i], load_sem.at[i]))
-    fields = []
-    for i, (source, target) in enumerate(((params_hbm, params), (side_hbm, side), (prior_hbm, prior))):
-        for c in range(2):
-            fields.append(
-                pltpu.make_async_copy(
-                    source.at[pl.ds(10 * c, 10), 0, :], target.at[pl.ds(16 * c, 10), :], field_sem.at[2 * i + c]
-                )
-            )
+    fields = [
+        pltpu.make_async_copy(source.at[:, :, 0, :], target.at[:, pl.ds(0, 10), :], field_sem.at[i])
+        for i, (source, target) in enumerate(((params_hbm, params), (side_hbm, side), (prior_hbm, prior)))
+    ]
     for target in (params, side, prior):
-        for c in range(2):
-            target[16 * c + 10 : 16 * c + 16, :] = jnp.zeros((6, TILES), F32)
+        target[:, 10:16, :] = jnp.zeros((2, 6, TILES), F32)
     small = [
         pltpu.make_async_copy(source, target, small_sem.at[i])
         for i, (source, target) in enumerate(
             ((lists_hbm, lists_ref), (count_hbm, count_ref), (first_hbm, first_ref), (second_hbm, second_ref))
         )
     ]
-    for copy in fields[:2] + small[:1] + loads[:1] + small[1:2] + loads[1:] + small[2:] + fields[2:]:
+    for copy in loads[:1] + small[:1] + fields[:1] + small[1:2] + loads[1:] + small[2:] + fields[1:]:
         copy.start()
 
+    halo_in[...] = jnp.zeros_like(halo_in)
+    fold_in[...] = jnp.zeros_like(fold_in)
+    lists_in[...] = jnp.zeros_like(lists_in)
     barrier = pltpu.get_barrier_semaphore()
     for peer in borrowers + owners[:2] + line + plane:
         pl.semaphore_signal(barrier, inc=1, device_id=peer, device_id_type=MESH)
 
+    above = [sec < secs - 1, sec < secs - 2, reg < regs - 1, reg > 0]
+    below = [sec > 0, sec > 1, reg > 0, reg < regs - 1]
     sent = []
 
-    def send(source, target, send_sem, recv_sem, peer):
+    def send(source, target, send_sem, recv_sem, peer, sends=None, receives=None):
         copy = pltpu.make_async_remote_copy(
             src_ref=source, dst_ref=target, send_sem=send_sem, recv_sem=recv_sem, device_id=peer, device_id_type=MESH
         )
-        copy.start()
-        sent.append(copy)
-        return copy
+        if sends is None:
+            copy.start()
+            sent.append(copy.wait_send)
+            return copy.wait_recv
+        pl.when(sends)(copy.start)
+        sent.append(lambda: pl.when(sends)(copy.wait_send))
+        return lambda: pl.when(receives)(copy.wait_recv)
 
     def send_halo(source, turn):
         return [
-            send(source, halo_in.at[turn, i], halo_send.at[turn, i], halo_recv.at[turn, i], borrowers[i])
+            send(
+                source.at[:, pl.ds(0, 10), :], halo_in.at[turn, i, :, pl.ds(0, 10), :], halo_send.at[turn, i], halo_recv.at[turn, i], borrowers[i], above[i], below[i]
+            )
             for i in range(4)
         ]
 
     def send_fold(turn):
         return [
-            send(fold_out.at[turn, i], fold_in.at[turn, i], fold_send.at[turn, i], fold_recv.at[turn, i], owners[i])
+            send(
+                fold_out.at[turn, i, :, pl.ds(0, 10), :], fold_in.at[turn, i, :, pl.ds(0, 10), :], fold_send.at[turn, i], fold_recv.at[turn, i], owners[i],
+                below[i], above[i],
+            )
             for i in range(4)
         ]
 
@@ -205,16 +214,16 @@
         turn(tile, at)
         gram_of(tile, at)
 
-    for copy in small[1:] + fields[2:] + loads:
+    for copy in small[1:] + fields[1:] + loads:
         copy.wait()
     pl.loop(0, EARLY)(form)
-    for copy in fields[:2] + small[:1]:
+    for copy in fields[:1] + small[:1]:
         copy.wait()
     pl.semaphore_wait(barrier, 6 + len(line) + len(plane))
     halo = send_halo(params, 0)
     borders = [
-        send(lists_ref, lists_in.at[0], list_send.at[0], list_recv.at[0], borrowers[2]),
-        send(lists_ref, lists_in.at[1], list_send.at[1], list_recv.at[1], borrowers[3]),
+        send(lists_ref, lists_in.at[0], list_send.at[0], list_recv.at[0], borrowers[2], above[2], below[2]),
+        send(lists_ref, lists_in.at[1], list_send.at[1], list_recv.at[1], borrowers[3], above[3], below[3]),
     ]
 
 
@@ -222,8 +231,8 @@
     for tile in range(FORMED, chunks):
         turn(tile, tile % 2)
 
-    for copy in borders:
-        copy.wait_recv()
+    for arrived in borders:
+        arrived()
     second = second_ref[...]
     width = lists_ref.shape[1]
     index = jnp.where(second < 3 * TILES, second, -1).astype(F32)
@@ -243,9 +252,9 @@
         mine = thirds(field)
         own = joined(matmul(mine, own_hot[...]))
         other = matmul(mine, other_hot[:TILES, :])
-        for copy in halo:
-            copy.wait_recv()
-        others = jnp.concatenate([thirds(halo_in[turn, i]) for i in range(4)], axis=1)
+        for arrived in halo:
+            arrived()
+        others = jnp.concatenate([thirds(halo_in[turn, i].reshape(FIELD, TILES)) for i in range(4)], axis=1)
         other = joined(other + matmul(others, other_hot[TILES:, :]))
         z_ref[0] = own
         z_ref[1] = other
@@ -298,17 +307,17 @@
         others = thirds(other)
         lent = joined(matmul_t(others, other_hot[TILES:, :]))
         for i in range(4):
-            fold_out[turn, i] = lent[:, i * TILES : (i + 1) * TILES]
+            fold_out[turn, i] = lent[:, i * TILES : (i + 1) * TILES].reshape(2, FIELD // 2, TILES)
         fold = send_fold(turn)
         local = joined(matmul_t(thirds(own), own_hot[...]) + matmul_t(others, other_hot[:TILES, :]))
         return fold, local
 
     def folded(fold, local, turn):
-        for copy in fold:
-            copy.wait_recv()
-        return local + fold_in[turn, 0] + fold_in[turn, 1] + fold_in[turn, 2] + fold_in[turn, 3]
-
-    start = params[...]
+        for arrived in fold:
+            arrived()
+        return local + jnp.sum(fold_in[turn], axis=0).reshape(FIELD, TILES)
+
+    start = params[...].reshape(FIELD, TILES)
     gathered(start, 0, halo)
     for c in range(2):
         for half in range(2):
@@ -319,14 +328,14 @@
     fold, local = scattered(0)
     for tile in range(FORMED, chunks - 1):
         gram_of(tile, tile % 2)
-    local = local + prior[...] * start
-    residual = side[...] - folded(fold, local, 0)
-
-    direction[...] = residual
+    local = local + prior[...].reshape(FIELD, TILES) * start
+    residual = side[...].reshape(FIELD, TILES) - folded(fold, local, 0)
+
+    direction[...] = residual.reshape(2, FIELD // 2, TILES)
     halo = send_halo(direction, 1)
     gram_of(chunks - 1, (chunks - 1) % 2)
     squares = jnp.sum(residual * residual, keepdims=True)
-    damped = prior[...] * residual
+    damped = prior[...].reshape(FIELD, TILES) * residual
     gathered(residual, 1, halo)
     products(chunks)
     energy = scale * jnp.sum(y_ref[0] * z_ref[0] + y_ref[1] * z_ref[1], keepdims=True) + jnp.sum(damped * residual, keepdims=True)
@@ -346,18 +355,18 @@
     sums = send_part(0, line)
     fold, local = scattered(1)
     local = local + damped
-    for copy in sums:
-        copy.wait_recv()
+    for arrived in sums:
+        arrived()
     total = total + jnp.sum(part_in[0, : len(line), :], axis=0, keepdims=True)
     part[1, 0:1, :] = total
     sums = send_part(1, plane)
     image = folded(fold, local, 1)
-    for copy in sums:
-        copy.wait_recv()
+    for arrived in sums:
+        arrived()
     total = total + jnp.sum(part_in[1, : len(plane), :], axis=0, keepdims=True)
     alpha = total[:, 0:1] / total[:, LANES // 2 : LANES // 2 + 1]
-    for copy in sent:
-        copy.wait_send()
+    for left_here in sent:
+        left_here()
     answer = start + alpha * residual
     left = residual - alpha * image
     for c in range(2):
@@ -373,7 +382,7 @@
     chunks = pairs // LANES
     vmem = pl.BlockSpec(memory_space=pltpu.VMEM)
     hbm = pl.BlockSpec(memory_space=pltpu.HBM)
-    field = (FIELD, TILES)
+    field, split = (FIELD, TILES), (2, FIELD // 2, TILES)
     dma = pltpu.SemaphoreType.DMA
     answer, left = pl.pallas_call(
         functools.partial(kernel, sizes),
@@ -385,9 +394,9 @@
             pltpu.VMEM((1, pairs), jnp.int32),
             pltpu.VMEM((chunks, 1, LANES), jnp.int32),
             pltpu.VMEM((2, width), jnp.int32),
-            pltpu.VMEM(field, F32),
-            pltpu.VMEM(field, F32),
-            pltpu.VMEM(field, F32),
+            pltpu.VMEM(split, F32),
+            pltpu.VMEM(split, F32),
+            pltpu.VMEM(split, F32),
             pltpu.VMEM((chunks, LANES, 4, slots), BF16),
             pltpu.VMEM((2, 5, slots, LANES), F32),
             pltpu.VMEM((4 * LANES, 4 * LANES), BF16),
@@ -396,16 +405,16 @@
             pltpu.VMEM((5 * TILES, pairs), BF16),
             pltpu.VMEM((2, FIELD, pairs), F32),
             pltpu.VMEM((2, FIELD, pairs), F32),
-            pltpu.VMEM(field, F32),
+            pltpu.VMEM(split, F32),
             pltpu.VMEM((2, 2, width), jnp.int32),
-            pltpu.VMEM((2, 4, *field), F32),
-            pltpu.VMEM((2, 4, *field), F32),
-            pltpu.VMEM((2, 4, *field), F32),
+            pltpu.VMEM((2, 4, *split), F32),
+            pltpu.VMEM((2, 4, *split), F32),
+            pltpu.VMEM((2, 4, *split), F32),
             pltpu.VMEM((2, 8, LANES), F32),
             pltpu.VMEM((2, part_rows, LANES), F32),
             dma((chunks,)),
             dma((4,)),
-            dma((6,)),
+            dma((3,)),
             dma((2,)),
             dma((2,)),
             dma((2, 4)),
@@ -417,9 +426,9 @@
         ],
         compiler_params=pltpu.CompilerParams(collective_id=0, has_side_effects=True, vmem_limit_bytes=32 * 2**20),
     )(*[pltpu.with_memory_space_constraint(x, pltpu.HBM) for x in (
-        start_params.reshape(20, 1, TILES),
-        right_side.reshape(20, 1, TILES),
-        prior.reshape(20, 1, TILES),
+        start_params.reshape(2, 10, 1, TILES),
+        right_side.reshape(2, 10, 1, TILES),
+        prior.reshape(2, 10, 1, TILES),
         matches.reshape(pairs, 4, slots),
         pair_first.reshape(1, pairs),
         pair_second.reshape(1, pairs),

time: 37.7 us -> 37.3 us (0.989)
  no operation moved by 1% of the time
where the time goes in v4:
time: 37.3 us; the launch traced here: 37.2 us
  Pallas kernels  35.4 us (95%)
  local copies, waits for them, and re-layouts  1.22 us (3%)
  between operations  0.64 us (2%)
    pallas_call x1, Pallas kernels, on_device(): pl.pallas_call(functools.partial(kernel, sizes), out_shape=(jax.ShapeDtyp...  35.4 us
    unnamed x2, local copies, waits for them, and re-layouts  1.22 us

profile of v4, /device:TPU:1, one launch (start us, length us, event | category | flops | bytes accessed | tf_op | source)
XLA Modules:
  0.0 37.2 jit_solution(9722477273582096566)
XLA Ops:
  0.6 35.4 %shard_map.95 = (f32[20,128]{1,0:T(8,128)S(1)}, f32[20,128]{1,0:T(8,128)S(1)}) custom-call(f32[2,10,1,128]{3,2,1,0:T(1,128)} %bitcast.13, f32[2,10,1,128]{3,2,1,0:T(1,128)} %bitcast.14, f32[2,10,1,128]{3,2,1,0:T(1,128)} %bitcast.15, bf16[640,4,256]{2,1,0:T(4,128)(2,1)} %bitcast.12, s32[1,640]{1,0:T(1,128)} %bitcast.16, s32[1,640]{1,0:T(1,128)} %bitcast.17, ...), custom_call_target="tpu_custom_call" | custom-call | tf_op jit(solution)/shard_map/pallas_call | solution.py:387
  36.0 0.6 %copy.10 = f32[1,1,20,128]{3,1,2,0:T(1,128)} copy(f32[1,1,20,128]{3,2,1,0:T(8,128)S(1)} %bitcast.11) | data formatting | bytes 20480
  36.6 0.6 %copy.11 = f32[1,1,20,128]{3,1,2,0:T(1,128)} copy(f32[1,1,20,128]{3,2,1,0:T(8,128)S(1)} %bitcast.10) | data formatting | bytes 20480

commit v5 on v4

--- a/solution.py
+++ b/solution.py
@@ -121,18 +121,6 @@
     slots = matches_hbm.shape[2]
     chunks = pairs // LANES
     rows = secs // group
-
-    def device(by_sec, by_reg):
-        return (lax.rem(sec + by_sec + secs, secs), lax.rem(reg + by_reg + regs, regs))
-
-    borrowers = [device(1, 0), device(2, 0), device(0, 1), device(0, -1)]
-    owners = [device(-1, 0), device(-2, 0), device(0, -1), device(0, 1)]
-    base, place = group * (sec // group), lax.rem(sec, group)
-    line = [(base + lax.rem(place + j, group), reg) for j in sorted(range(1, group), key=lambda j: abs(2 * j - group))]
-    hops = [(min(a, rows - a) + min(b, regs - b), a, b) for a in range(rows) for b in range(regs) if a or b]
-    plane = [
-        (lax.rem(sec // group + a, rows) * group + place, lax.rem(reg + b, regs)) for _, a, b in sorted(hops, reverse=True)
-    ]
 
     loads = []
     for i in range(chunks):
@@ -152,6 +140,18 @@
     for copy in loads[:1] + small[:1] + fields[:1] + small[1:2] + loads[1:] + small[2:] + fields[1:]:
         copy.start()
 
+    def device(by_sec, by_reg):
+        return (lax.rem(sec + by_sec + secs, secs), lax.rem(reg + by_reg + regs, regs))
+
+    borrowers = [device(1, 0), device(2, 0), device(0, 1), device(0, -1)]
+    owners = [device(-1, 0), device(-2, 0), device(0, -1), device(0, 1)]
+    base, place = group * (sec // group), lax.rem(sec, group)
+    line = [(base + lax.rem(place + j, group), reg) for j in sorted(range(1, group), key=lambda j: abs(2 * j - group))]
+    hops = [(min(a, rows - a) + min(b, regs - b), a, b) for a in range(rows) for b in range(regs) if a or b]
+    plane = [
+        (lax.rem(sec // group + a, rows) * group + place, lax.rem(reg + b, regs)) for _, a, b in sorted(hops, reverse=True)
+    ]
+
     halo_in[...] = jnp.zeros_like(halo_in)
     fold_in[...] = jnp.zeros_like(fold_in)
     lists_in[...] = jnp.zeros_like(lists_in)
@@ -214,9 +214,11 @@
         turn(tile, at)
         gram_of(tile, at)
 
-    for copy in small[1:] + fields[1:] + loads:
+    for copy in small[1:2] + loads[:1]:
         copy.wait()
     pl.loop(0, EARLY)(form)
+    for copy in loads[1:] + small[2:] + fields[1:]:
+        copy.wait()
     for copy in fields[:1] + small[:1]:
         copy.wait()
     pl.semaphore_wait(barrier, 6 + len(line) + len(plane))
@@ -246,7 +248,7 @@
     column = lax.broadcasted_iota(jnp.int32, (TILES, pairs), 0)
     own_hot[...] = jnp.where(column == first_ref[...], 1.0, 0.0).astype(BF16)
     for i in range(5):
-        other_hot[i * TILES : (i + 1) * TILES, :] = jnp.where(column + i * TILES == index, -1.0, 0.0).astype(BF16)
+        other_hot[i * TILES : (i + 1) * TILES, :] = jnp.where(column == index - i * TILES, -1.0, 0.0).astype(BF16)
 
     def gathered(field, turn, halo):
         mine = thirds(field)
@@ -361,12 +363,12 @@
     part[1, 0:1, :] = total
     sums = send_part(1, plane)
     image = folded(fold, local, 1)
+    for left_here in sent:
+        left_here()
     for arrived in sums:
         arrived()
     total = total + jnp.sum(part_in[1, : len(plane), :], axis=0, keepdims=True)
     alpha = total[:, 0:1] / total[:, LANES // 2 : LANES // 2 + 1]
-    for left_here in sent:
-        left_here()
     answer = start + alpha * residual
     left = residual - alpha * image
     for c in range(2):

time: 37.3 us -> 36.9 us (0.989)
  Pallas kernels: 35.4 us -> 34.9 us
    pallas_call x1, Pallas kernels: 35.4 us -> 34.9 us  [on_device(): pl.pallas_call(functools.partial(kernel, sizes), out_shape=(jax.ShapeDtyp...]
where the time goes in v5:
time: 36.9 us; the launch traced here: 36.8 us
  Pallas kernels  34.9 us (95%)
  local copies, waits for them, and re-layouts  1.22 us (3%)
  between operations  0.64 us (2%)
    pallas_call x1, Pallas kernels, on_device(): pl.pallas_call(functools.partial(kernel, sizes), out_shape=(jax.ShapeDtyp...  34.9 us
    unnamed x2, local copies, waits for them, and re-layouts  1.22 us

profile of v5, /device:TPU:1, one launch (start us, length us, event | category | flops | bytes accessed | tf_op | source)
XLA Modules:
  0.0 36.8 jit_solution(12579251029017319862)
XLA Ops:
  0.6 34.9 %shard_map.95 = (f32[20,128]{1,0:T(8,128)S(1)}, f32[20,128]{1,0:T(8,128)S(1)}) custom-call(f32[2,10,1,128]{3,2,1,0:T(1,128)} %bitcast.13, f32[2,10,1,128]{3,2,1,0:T(1,128)} %bitcast.14, f32[2,10,1,128]{3,2,1,0:T(1,128)} %bitcast.15, bf16[640,4,256]{2,1,0:T(4,128)(2,1)} %bitcast.12, s32[1,640]{1,0:T(1,128)} %bitcast.16, s32[1,640]{1,0:T(1,128)} %bitcast.17, ...), custom_call_target="tpu_custom_call" | custom-call | tf_op jit(solution)/shard_map/pallas_call | solution.py:389
  35.5 0.6 %copy.10 = f32[1,1,20,128]{3,1,2,0:T(1,128)} copy(f32[1,1,20,128]{3,2,1,0:T(8,128)S(1)} %bitcast.11) | data formatting | bytes 20480
  36.2 0.6 %copy.11 = f32[1,1,20,128]{3,1,2,0:T(1,128)} copy(f32[1,1,20,128]{3,2,1,0:T(8,128)S(1)} %bitcast.10) | data formatting | bytes 20480

commit v6 on v5

--- a/solution.py
+++ b/solution.py
@@ -16,7 +16,7 @@
 FIELD = 32
 UNROLL = 16
 EARLY = 1
-FORMED = 3
+FORMED = 2
 GROUPS = ((1, 2, 3), (4, 5, 6), (7, 8, 9))
 
 
@@ -210,7 +210,7 @@
         gram_tile(coords.at[at], gram, tile, count_ref[tile].astype(F32), slots)
 
     def form(tile):
-        at = lax.rem(tile, 2)
+        at = lax.rem(tile, 3)
         turn(tile, at)
         gram_of(tile, at)
 
@@ -231,7 +231,7 @@
 
     pl.loop(EARLY, FORMED)(form)
     for tile in range(FORMED, chunks):
-        turn(tile, tile % 2)
+        turn(tile, tile % 3)
 
     for arrived in borders:
         arrived()
@@ -279,7 +279,7 @@
 
     def direct(tile):
         at = slice(tile * LANES, (tile + 1) * LANES)
-        points_of = coords.at[tile % 2]
+        points_of = coords.at[tile % 3]
         for c in range(2):
             z = [[z_ref[half, 16 * c + m : 16 * c + m + 1, at] for m in range(10)] for half in range(2)]
             constant = z[0][0] + z[1][0]
@@ -328,14 +328,15 @@
         direct(tile)
     products(FORMED)
     fold, local = scattered(0)
-    for tile in range(FORMED, chunks - 1):
-        gram_of(tile, tile % 2)
+    for tile in range(FORMED, chunks - 2):
+        gram_of(tile, tile % 3)
     local = local + prior[...].reshape(FIELD, TILES) * start
     residual = side[...].reshape(FIELD, TILES) - folded(fold, local, 0)
 
     direction[...] = residual.reshape(2, FIELD // 2, TILES)
     halo = send_halo(direction, 1)
-    gram_of(chunks - 1, (chunks - 1) % 2)
+    gram_of(chunks - 2, (chunks - 2) % 3)
+    gram_of(chunks - 1, (chunks - 1) % 3)
     squares = jnp.sum(residual * residual, keepdims=True)
     damped = prior[...].reshape(FIELD, TILES) * residual
     gathered(residual, 1, halo)
@@ -400,7 +401,7 @@
             pltpu.VMEM(split, F32),
             pltpu.VMEM(split, F32),
             pltpu.VMEM((chunks, LANES, 4, slots), BF16),
-            pltpu.VMEM((2, 5, slots, LANES), F32),
+            pltpu.VMEM((3, 5, slots, LANES), F32),
             pltpu.VMEM((4 * LANES, 4 * LANES), BF16),
             pltpu.VMEM((chunks, 20, FIELD, LANES), F32),
             pltpu.VMEM((TILES, pairs), BF16),

time: 36.9 us -> 36.1 us (0.978)
  Pallas kernels: 34.9 us -> 34.1 us
    pallas_call x1, Pallas kernels: 34.9 us -> 34.1 us  [on_device(): pl.pallas_call(functools.partial(kernel, sizes), out_shape=(jax.ShapeDtyp...]
where the time goes in v6:
time: 36.1 us; the launch traced here: 36 us
  Pallas kernels  34.1 us (94%)
  local copies, waits for them, and re-layouts  1.22 us (3%)
  between operations  0.64 us (2%)
    pallas_call x1, Pallas kernels, on_device(): pl.pallas_call(functools.partial(kernel, sizes), out_shape=(jax.ShapeDtyp...  34.1 us
    unnamed x2, local copies, waits for them, and re-layouts  1.22 us

profile of v6, /device:TPU:1, one launch (start us, length us, event | category | flops | bytes accessed | tf_op | source)
XLA Modules:
  0.0 36.0 jit_solution(7345745511496338440)
XLA Ops:
  0.6 34.1 %shard_map.95 = (f32[20,128]{1,0:T(8,128)S(1)}, f32[20,128]{1,0:T(8,128)S(1)}) custom-call(f32[2,10,1,128]{3,2,1,0:T(1,128)} %bitcast.13, f32[2,10,1,128]{3,2,1,0:T(1,128)} %bitcast.14, f32[2,10,1,128]{3,2,1,0:T(1,128)} %bitcast.15, bf16[640,4,256]{2,1,0:T(4,128)(2,1)} %bitcast.12, s32[1,640]{1,0:T(1,128)} %bitcast.16, s32[1,640]{1,0:T(1,128)} %bitcast.17, ...), custom_call_target="tpu_custom_call" | custom-call | tf_op jit(solution)/shard_map/pallas_call | solution.py:390
  34.7 0.6 %copy.10 = f32[1,1,20,128]{3,1,2,0:T(1,128)} copy(f32[1,1,20,128]{3,2,1,0:T(8,128)S(1)} %bitcast.11) | data formatting | bytes 20480
  35.4 0.6 %copy.11 = f32[1,1,20,128]{3,1,2,0:T(1,128)} copy(f32[1,1,20,128]{3,2,1,0:T(8,128)S(1)} %bitcast.10) | data formatting | bytes 20480

commit v7 on v6

--- a/solution.py
+++ b/solution.py
@@ -156,7 +156,7 @@
     fold_in[...] = jnp.zeros_like(fold_in)
     lists_in[...] = jnp.zeros_like(lists_in)
     barrier = pltpu.get_barrier_semaphore()
-    for peer in borrowers + owners[:2] + line + plane:
+    for peer in [p for both in zip(line, plane) for p in both] + line[len(plane) :] + plane[len(line) :] + borrowers + owners[:2]:
         pl.semaphore_signal(barrier, inc=1, device_id=peer, device_id_type=MESH)
 
     above = [sec < secs - 1, sec < secs - 2, reg < regs - 1, reg > 0]

time: 36.1 us -> 36 us (level)
  no operation moved by 1% of the time
where the time goes in v7:
time: 36 us; the launch traced here: 35.9 us
  Pallas kernels  34 us (94%)
  local copies, waits for them, and re-layouts  1.22 us (3%)
  between operations  0.64 us (2%)
    pallas_call x1, Pallas kernels, on_device(): pl.pallas_call(functools.partial(kernel, sizes), out_shape=(jax.ShapeDtyp...  34 us
    unnamed x2, local copies, waits for them, and re-layouts  1.22 us

profile of v7, /device:TPU:1, one launch (start us, length us, event | category | flops | bytes accessed | tf_op | source)
XLA Modules:
  0.0 35.9 jit_solution(10288570181417580927)
XLA Ops:
  0.6 34.0 %shard_map.95 = (f32[20,128]{1,0:T(8,128)S(1)}, f32[20,128]{1,0:T(8,128)S(1)}) custom-call(f32[2,10,1,128]{3,2,1,0:T(1,128)} %bitcast.13, f32[2,10,1,128]{3,2,1,0:T(1,128)} %bitcast.14, f32[2,10,1,128]{3,2,1,0:T(1,128)} %bitcast.15, bf16[640,4,256]{2,1,0:T(4,128)(2,1)} %bitcast.12, s32[1,640]{1,0:T(1,128)} %bitcast.16, s32[1,640]{1,0:T(1,128)} %bitcast.17, ...), custom_call_target="tpu_custom_call" | custom-call | tf_op jit(solution)/shard_map/pallas_call | solution.py:390
  34.7 0.6 %copy.10 = f32[1,1,20,128]{3,1,2,0:T(1,128)} copy(f32[1,1,20,128]{3,2,1,0:T(8,128)S(1)} %bitcast.11) | data formatting | bytes 20480
  35.3 0.6 %copy.11 = f32[1,1,20,128]{3,1,2,0:T(1,128)} copy(f32[1,1,20,128]{3,2,1,0:T(8,128)S(1)} %bitcast.10) | data formatting | bytes 20480
